TPU v7x, 32 devices: a whole 2x2x4 slice. The times are simulated.
32 devices in a mesh: wide: 4 (over z), blk: 8 (over y, x, core).
Axes of the slice: x: 2, y: 2, z: 4, core: 2. Of those that a mesh axis runs over, the one named last changes fastest.
Arguments:
- rhs: float32 [131072, 256], P(('wide', 'blk'))
- near_blocks: bfloat16 [131072, 1536], P(('wide', 'blk')), may hold values from -0.078125 to 0.078125
- source_basis: bfloat16 [131072, 64], P(('wide', 'blk')), may hold values from -0.5 to 0.5
- target_basis: bfloat16 [131072, 64], P(('wide', 'blk')), may hold values from -0.375 to 0.375
- far_coupling: bfloat16 [1024, 1, 64, 64], P(('wide', 'blk')), may hold values from -0.75 to 0.75
- send_ids: int32 [32, 32, 1], P(('wide', 'blk')), may hold values from 0 to 31
- far_list: int32 [32, 32], P(('wide', 'blk')), may hold values from 0 to 31, each once within a row
Outputs:
- solution: float32 [131072, 256], P(('wide', 'blk'))
- residual: float32 [131072, 256], P(('wide', 'blk'))
Inputs may be any that keep to these rules, and one draw needn't show every extreme that they name: Each row of far_list names each received slot 0 to 31 exactly once.
All inputs are finite; a program needn't handle non-finite values.
Results may differ from a plain program's by a relative error of at most 0.0035.
The roundings to bfloat16 on the way count: a program that leaves them out, or rounds other values in their place, can miss the bound.
Values may be sent and summed in bfloat16 or wider, within the bound.
A program may use at most 128 MiB of HBM per device.

v0:
```python
import jax
import jax.numpy as jnp
from jax import lax
from jax.sharding import PartitionSpec as P

NEAR = 1024
HALO = 256
LEAF = 128
ITERS = 2


def with_halo(value, sides, width):
    for axis, dim in sides:
        count, length = (lax.axis_size(axis), value.shape[dim])
        up = [(i, (i + 1) % count) for i in range(count)]
        down = [(j, i) for i, j in up]
        last = lax.slice_in_dim(value, length - width, length, axis=dim)
        first = lax.slice_in_dim(value, 0, width, axis=dim)
        before = lax.ppermute(last, axis, up)
        after = lax.ppermute(first, axis, down)
        value = jnp.concatenate([before, value, after], axis=dim)
    return value


def near_apply(near_rows, ext):
    outs = []
    for j in range(near_rows.shape[0] // NEAR):
        outs.append(
            jnp.dot(
                near_rows[j * NEAR : (j + 1) * NEAR],
                ext[j * NEAR : j * NEAR + NEAR + 2 * HALO],
                preferred_element_type=jnp.float32,
            )
        )
    return jnp.concatenate(outs, axis=0)


def shards(rhs, near_blocks, source_basis, target_basis, far_coupling, send_ids, far_list):
    rows, width = rhs.shape
    rank = source_basis.shape[1]
    leaves = rows // LEAF
    fanout = far_list.shape[1] // leaves
    senders = send_ids[0].reshape(-1)
    readers = far_list[0]
    source_leaf = source_basis.reshape(leaves, LEAF, rank)
    target_leaf = target_basis.reshape(leaves, LEAF, rank)
    solution = jnp.zeros_like(rhs)
    residual = rhs
    for step in range(ITERS):
        vb = residual.astype(jnp.bfloat16)
        ext = with_halo(vb, (("blk", 0),), HALO)
        coef = jnp.einsum(
            "lia,lis->las",
            source_leaf,
            vb.reshape(leaves, LEAF, width),
            preferred_element_type=jnp.float32,
        ).astype(jnp.bfloat16)
        outgoing = coef[senders]
        incoming = lax.all_to_all(
            outgoing, ("wide", "blk"), split_axis=0, concat_axis=0, tiled=True
        )
        near = near_apply(near_blocks, ext)
        picked = incoming[readers].reshape(leaves, fanout, rank, width)
        trans = jnp.einsum(
            "lfab,lfbs->las", far_coupling, picked, preferred_element_type=jnp.float32
        ).astype(jnp.bfloat16)
        far = jnp.einsum(
            "lia,las->lis", target_leaf, trans, preferred_element_type=jnp.float32
        ).reshape(rows, width)
        image = residual + near + far
        local_gram = jnp.einsum("rs,rt->st", image, image, precision=lax.Precision.HIGHEST)
        local_proj = jnp.einsum("rs,rt->st", image, residual, precision=lax.Precision.HIGHEST)
        gram, proj = lax.psum((local_gram, local_proj), ("wide", "blk"))
        factor = jnp.linalg.cholesky(gram)
        alpha = jax.scipy.linalg.cho_solve((factor, True), proj)
        solution = solution + jnp.dot(residual, alpha, precision=lax.Precision.HIGHEST)
        residual = residual - jnp.dot(image, alpha, precision=lax.Precision.HIGHEST)
    return (solution, residual)


def solution(mesh):
    in_specs = (
        P(("wide", "blk"), None),
        P(("wide", "blk"), None),
        P(("wide", "blk"), None),
        P(("wide", "blk"), None),
        P(("wide", "blk"), None, None, None),
        P(("wide", "blk"), None, None),
        P(("wide", "blk"), None),
    )
    out_specs = (P(("wide", "blk"), None), P(("wide", "blk"), None))
    return jax.shard_map(shards, mesh=mesh, in_specs=in_specs, out_specs=out_specs, check_vma=False)
```

profile of v0, /device:TPU:29, one launch (start us, length us, event | category | flops | bytes accessed | tf_op | source)
XLA Modules:
  0.0 554.1 jit_solution(8985881186335456876)
XLA Ops:
  7.2 2.5 convert_element_type.23
  9.7 1.4 convolution_convert_fusion.1
  11.1 2.8 gather_fusion
  13.9 6.2 %all-to-all-start = ((bf16[32,64,256]{2,1,0:T(8,128)(2,1)}), bf16[32,64,256]{2,1,0:T(8,128)(2,1)}, u32[]{:S(2)}, u32[]{:S(2)}) async-start(bf16[32,64,256]{2,1,0:T(8,128)(2,1)} %gather_fusion), calls=%async_computation | async-start | bytes 2097152 | tf_op jit(solution)/shard_map/all_to_all | solution.py:59
  20.2 1.5 collective-permute-start
  21.7 3.9 fusion.12
  25.6 3.9 fusion.8
  29.6 5.6 %copy.43 = f32[4096,256]{0,1:T(8,128)} copy(f32[4096,256]{1,0:T(8,128)} %param.10) | data formatting | bytes 8388608 | tf_op args[0]
  35.2 4.0 fusion.21
  39.3 4.0 fusion.33
  43.2 0.9 all-to-all-done
  44.1 1.8 gather_fusion.1
  46.0 4.0 fusion.19
  50.0 5.7 %copy.68 = f32[4096,256]{0,1:T(8,128)} copy(f32[4096,256]{1,0:T(8,128)} %bitcast.152) | data formatting | bytes 8388608 | tf_op jit(solution)/shard_map/reshape | solution.py:69
  55.7 4.8 fusion
  60.5 4.2 fusion.96
  64.8 4.4 fusion.97
  69.2 127.4 %all-reduce.8.cloned.1.call-done = (f32[256,256]{1,0:T(8,128)}, f32[256,256]{0,1:T(8,128)}) async-done(((f32[256,256]{1,0:T(8,128)}, f32[256,256]{0,1:T(8,128)}), (f32[256,256]{1,0:T(8,128)}, f32[256,256]{0,1:T(8,128)})) %all-reduce.8.cloned.1.call-update) | async-done | bytes 524304 | tf_op jit(solution)/shard_map/psum | solution.py:73
  196.6 1.1 copy.48
  197.7 1.0 fusion.60
  198.7 11.7 %cholesky.130 = f32[128,128]{1,0:T(8,128)S(1)} custom-call(f32[128,128]{1,0:T(8,128)S(1)} %cholesky.194), custom_call_target="Cholesky" | custom-call | tf_op jit(solution)/shard_map/jit(cholesky)/cholesky | solution.py:74
  210.5 10.0 %custom-call.15 = f32[1,128,128]{1,2,0:T(8,128)S(1)} custom-call(f32[1,128,128]{2,1,0:T(8,128)S(1)} %get-tuple-element.61), custom_call_target="InvertDiagBlocksLowerTriangular" | custom-call | tf_op jit(solution)/shard_map/jit(cholesky)/cholesky | solution.py:74
  220.9 11.7 %cholesky.147 = f32[128,128]{1,0:T(8,128)S(1)} custom-call(f32[128,128]{1,0:T(8,128)S(1)} %convolution_subtract_fusion.7), custom_call_target="Cholesky" | custom-call | tf_op jit(solution)/shard_map/jit(cholesky)/cholesky | solution.py:74
  232.7 0.7 compare_reduce_fusion.2
  234.8 3.9 while.4
  234.8 0.6 fusion.136
  235.4 1.3 bitcast_dynamic-update-slice_fusion.4
  237.3 1.3 bitcast_dynamic-update-slice_fusion.4
  238.7 19.9 %custom-call.16 = f32[2,128,128]{1,2,0:T(8,128)S(1)} custom-call(f32[2,128,128]{2,1,0:T(8,128)S(1)} %get-tuple-element.18), custom_call_target="InvertDiagBlocksLowerTriangular" | custom-call | tf_op jit(solution)/shard_map/jit(_cho_solve)/triangular_solve | solution.py:75
  258.6 1.2 fusion.63
  261.2 12.1 %fusion.95 = (bf16[4096,256]{1,0:T(8,128)(2,1)S(1)}, f32[4096,256]{1,0:T(8,128)}) fusion(f32[4096,256]{1,0:T(8,128)} %param.10, f32[4096,256]{0,1:T(8,128)} %copy-done.4, f32[128,256]{1,0:T(8,128)S(1)} %fusion.72, f32[128,256]{1,0:T(8,128)S(1)} %fusion.71), kind=kOutput, calls=%fused_computation.141 | convolution fusion | flops 3223388160 | bytes 14942208 | tf_op jit(solution)/shard_map/dot_general | solution.py:77
  273.4 1.4 fusion.18
  274.8 2.9 gather_fusion.2
  277.7 7.0 %all-to-all-start.1 = ((bf16[32,64,256]{2,1,0:T(8,128)(2,1)}), bf16[32,64,256]{2,1,0:T(8,128)(2,1)}, u32[]{:S(2)}, u32[]{:S(2)}) async-start(bf16[32,64,256]{2,1,0:T(8,128)(2,1)} %gather_fusion.2), calls=%async_computation.1 | async-start | bytes 2097152 | tf_op jit(solution)/shard_map/all_to_all | solution.py:59
  284.8 1.5 collective-permute-start.2
  286.3 3.8 fusion.27
  290.1 3.9 fusion.30
  294.0 0.6 collective-permute-done.2
  294.6 3.9 fusion.24
  298.9 3.8 fusion.36
  302.7 5.9 %all-to-all-done.1 = bf16[32,64,256]{2,1,0:T(8,128)(2,1)} async-done(((bf16[32,64,256]{2,1,0:T(8,128)(2,1)}), bf16[32,64,256]{2,1,0:T(8,128)(2,1)}, u32[]{:S(2)}, u32[]{:S(2)}) %all-to-all-start.1) | async-done | bytes 1048608 | tf_op jit(solution)/shard_map/all_to_all | solution.py:59
  308.7 1.8 gather_fusion.3
  310.5 3.0 fusion.20
  313.5 5.2 fusion.1
  318.7 7.7 %fusion.98 = f32[256,256]{0,1:T(8,128)} fusion(f32[4096,256]{1,0:T(8,128)S(1)} %fusion.1), kind=kOutput, calls=%fused_computation.144 | convolution fusion | flops 3221225472 | bytes 4456448 | tf_op jit(solution)/shard_map/rs,rt->st/dot_general | solution.py:71
  326.4 7.9 %fusion.99 = f32[256,256]{1,0:T(8,128)} fusion(f32[4096,256]{1,0:T(8,128)S(1)} %fusion.1, f32[4096,256]{1,0:T(8,128)S(1)} %copy-done.2), kind=kOutput, calls=%fused_computation.145 | convolution fusion | flops 3221225472 | bytes 8650752 | tf_op jit(solution)/shard_map/rs,rt->st/dot_general | solution.py:72
  334.3 12.6 %convolution_bitcast_fusion = f32[4096,256]{0,1:T(8,128)} fusion(f32[4096,256]{1,0:T(8,128)} %param.10, f32[128,256]{1,0:T(8,128)S(1)} %fusion.72, f32[128,256]{1,0:T(8,128)S(1)} %fusion.71), kind=kOutput, calls=%fused_computation.11 | convolution fusion | flops 3221291008 | bytes 8650752 | tf_op jit(solution)/shard_map/dot_general | solution.py:76
  346.9 114.9 %all-reduce.6.cloned.1.call-done = (f32[256,256]{1,0:T(8,128)}, f32[256,256]{0,1:T(8,128)}) async-done(((f32[256,256]{1,0:T(8,128)}, f32[256,256]{0,1:T(8,128)}), (f32[256,256]{1,0:T(8,128)}, f32[256,256]{0,1:T(8,128)})) %all-reduce.6.cloned.1.call-update) | async-done | bytes 524304 | tf_op jit(solution)/shard_map/psum | solution.py:73
  461.8 1.1 copy.56
  462.9 1.0 fusion.59
  463.9 11.7 %cholesky.164 = f32[128,128]{1,0:T(8,128)S(1)} custom-call(f32[128,128]{1,0:T(8,128)S(1)} %cholesky.197), custom_call_target="Cholesky" | custom-call | tf_op jit(solution)/shard_map/jit(cholesky)/cholesky | solution.py:74
  475.7 9.8 %custom-call.17 = f32[1,128,128]{1,2,0:T(8,128)S(1)} custom-call(f32[1,128,128]{2,1,0:T(8,128)S(1)} %get-tuple-element.57), custom_call_target="InvertDiagBlocksLowerTriangular" | custom-call | tf_op jit(solution)/shard_map/jit(cholesky)/cholesky | solution.py:74
  486.0 11.7 %cholesky.181 = f32[128,128]{1,0:T(8,128)S(1)} custom-call(f32[128,128]{1,0:T(8,128)S(1)} %convolution_subtract_fusion.6), custom_call_target="Cholesky" | custom-call | tf_op jit(solution)/shard_map/jit(cholesky)/cholesky | solution.py:74
  497.7 0.7 compare_reduce_fusion
  498.4 0.6 compare_reduce_fusion.1
  500.4 4.0 while.5
  501.0 1.4 bitcast_dynamic-update-slice_fusion.5
  502.4 0.6 fusion.137
  503.0 1.4 bitcast_dynamic-update-slice_fusion.5
  504.4 19.9 %custom-call.18 = f32[2,128,128]{1,2,0:T(8,128)S(1)} custom-call(f32[2,128,128]{2,1,0:T(8,128)S(1)} %get-tuple-element.19), custom_call_target="InvertDiagBlocksLowerTriangular" | custom-call | tf_op jit(solution)/shard_map/jit(_cho_solve)/triangular_solve | solution.py:75
  524.3 1.2 fusion.61
  527.0 9.0 %convolution_subtract_fusion = f32[4096,256]{1,0:T(8,128)} fusion(f32[4096,256]{1,0:T(8,128)} %get-tuple-element.65, f32[4096,256]{1,0:T(8,128)} %copy-done.5, f32[128,256]{1,0:T(8,128)S(1)} %fusion.75, f32[128,256]{1,0:T(8,128)S(1)} %fusion.74), kind=kOutput, calls=%fused_computation.8 | convolution fusion | flops 3222339584 | bytes 12845056 | tf_op jit(solution)/shard_map/dot_general | solution.py:77
  536.0 5.4 convolution_add_fusion
  541.4 5.6 %copy.58 = f32[4096,256]{1,0:T(8,128)} copy(f32[4096,256]{0,1:T(8,128)} %convolution_add_fusion) | data formatting | bytes 8388608
  (81 shorter events, 5.9 us)
Async XLA Ops:
  7.2 38.8 %copy-start = (bf16[32,1,64,64]{3,2,1,0:T(8,128)(2,1)S(1)}, bf16[32,1,64,64]{3,2,1,0:T(8,128)(2,1)}, u32[]{:S(2)}) copy-start(bf16[32,1,64,64]{3,2,1,0:T(8,128)(2,1)} %param.14) | copy-start | bytes 786436
  7.2 2.5 copy-start.14
  7.2 2.5 copy-start.7
  13.9 30.2 %all-to-all-start = ((bf16[32,64,256]{2,1,0:T(8,128)(2,1)}), bf16[32,64,256]{2,1,0:T(8,128)(2,1)}, u32[]{:S(2)}, u32[]{:S(2)}) async-start(bf16[32,64,256]{2,1,0:T(8,128)(2,1)} %gather_fusion), calls=%async_computation | async-start | bytes 2097152 | tf_op jit(solution)/shard_map/all_to_all | solution.py:59
  20.1 176.5 %all-reduce.8.cloned.1.call-start = ((), (), s32[]{:S(2)}) async-start(), calls=%async_computation.3 | async-start | bytes 1048576 | tf_op jit(solution)/shard_map/psum | solution.py:73
  20.2 15.0 %collective-permute-start = (bf16[256,256]{1,0:T(8,128)(2,1)S(1)}, bf16[256,256]{1,0:T(8,128)(2,1)}, u32[]{:S(2)}, u32[]{:S(2)}) collective-permute-start(bf16[256,256]{1,0:T(8,128)(2,1)S(1)} %get-tuple-element.52), channel_id=1, source_target_pairs={{0,1},{1,2},{2,3},{3,4},{4,5},{5,6},{6,7},{7,0},{8,9},{9,10},{10,1... | collective-permute-start | bytes 393224 | tf_op jit(solution)/shard_map/ppermute | solution.py:19
  21.7 17.5 %collective-permute-start.1 = (bf16[256,256]{1,0:T(8,128)(2,1)S(1)}, bf16[256,256]{1,0:T(8,128)(2,1)S(1)}, u32[]{:S(2)}, u32[]{:S(2)}) collective-permute-start(bf16[256,256]{1,0:T(8,128)(2,1)S(1)} %get-tuple-element.53), channel_id=1, source_target_pairs={{1,0},{2,1},{3,2},{4,3},{5,4},{6,5},{7,6},{0,7},{9,8},{10,9},{11,1... | collective-permute-start | bytes 393224 | tf_op jit(solution)/shard_map/ppermute | solution.py:20
  25.6 3.9 copy-start.15
  50.0 5.7 %copy-start.10 = (f32[1024,256]{0,1:T(8,128)S(1)}, f32[1024,256]{0,1:T(8,128)}, u32[]{:S(2)}) copy-start(f32[1024,256]{0,1:T(8,128)} %fusion.12) | copy-start | bytes 3145732
  50.0 5.7 %copy-start.11 = (f32[1024,256]{0,1:T(8,128)S(1)}, f32[1024,256]{0,1:T(8,128)}, u32[]{:S(2)}) copy-start(f32[1024,256]{0,1:T(8,128)} %fusion.8) | copy-start | bytes 3145732
  60.5 4.3 copy-start.4
  60.5 4.2 copy-start.1
  196.6 63.2 %copy-start.12 = (f32[256,256]{1,0:T(8,128)S(1)}, f32[256,256]{1,0:T(8,128)}, u32[]{:S(2)}) copy-start(f32[256,256]{1,0:T(8,128)} %get-tuple-element.44) | copy-start | bytes 786436
  277.7 31.0 %all-to-all-start.1 = ((bf16[32,64,256]{2,1,0:T(8,128)(2,1)}), bf16[32,64,256]{2,1,0:T(8,128)(2,1)}, u32[]{:S(2)}, u32[]{:S(2)}) async-start(bf16[32,64,256]{2,1,0:T(8,128)(2,1)} %gather_fusion.2), calls=%async_computation.1 | async-start | bytes 2097152 | tf_op jit(solution)/shard_map/all_to_all | solution.py:59
  284.7 177.1 %all-reduce.6.cloned.1.call-start = ((), (), s32[]{:S(2)}) async-start(), calls=%async_computation.2 | async-start | bytes 1048576 | tf_op jit(solution)/shard_map/psum | solution.py:73
  284.8 9.9 %collective-permute-start.2 = (bf16[256,256]{1,0:T(8,128)(2,1)S(1)}, bf16[256,256]{1,0:T(8,128)(2,1)S(1)}, u32[]{:S(2)}, u32[]{:S(2)}) collective-permute-start(bf16[256,256]{1,0:T(8,128)(2,1)S(1)} %get-tuple-element.50), channel_id=1, source_target_pairs={{0,1},{1,2},{2,3},{3,4},{4,5},{5,6},{6,7},{7,0},{8,9},{9,10},{10,1... | collective-permute-start | bytes 393224 | tf_op jit(solution)/shard_map/ppermute | solution.py:19
  294.0 4.9 collective-permute-start.3
  298.5 12.0 %copy-start.8 = (bf16[4096,64]{0,1:T(8,128)(2,1)S(1)}, bf16[4096,64]{0,1:T(8,128)(2,1)}, u32[]{:S(2)}) copy-start(bf16[4096,64]{0,1:T(8,128)(2,1)} %param.13) | copy-start | bytes 1572868
  302.7 10.8 %copy-start.9 = (f32[1024,256]{1,0:T(8,128)S(1)}, f32[1024,256]{1,0:T(8,128)}, u32[]{:S(2)}) copy-start(f32[1024,256]{1,0:T(8,128)} %fusion.27) | copy-start | bytes 3145732
  318.7 7.7 %copy-start.5 = (f32[4096,256]{1,0:T(8,128)}, f32[4096,256]{1,0:T(8,128)S(1)}, u32[]{:S(2)}) copy-start(f32[4096,256]{1,0:T(8,128)S(1)} %fusion.1) | copy-start | bytes 12582916
  318.7 7.7 %copy-start.2 = (f32[4096,256]{1,0:T(8,128)S(1)}, f32[4096,256]{1,0:T(8,128)}, u32[]{:S(2)}) copy-start(f32[4096,256]{1,0:T(8,128)} %get-tuple-element.65) | copy-start | bytes 12582916
  461.8 63.7 %copy-start.13 = (f32[256,256]{1,0:T(8,128)S(1)}, f32[256,256]{1,0:T(8,128)}, u32[]{:S(2)}) copy-start(f32[256,256]{1,0:T(8,128)} %get-tuple-element.42) | copy-start | bytes 786436
  526.9 9.1 %copy-start.3 = (f32[4096,256]{1,0:T(8,128)S(1)}, f32[4096,256]{1,0:T(8,128)}, u32[]{:S(2)}) copy-start(f32[4096,256]{1,0:T(8,128)} %get-tuple-element.65) | copy-start | bytes 12582916
  526.9 9.1 %copy-start.6 = (f32[4096,256]{0,1:T(8,128)S(1)}, f32[4096,256]{0,1:T(8,128)}, u32[]{:S(2)}) copy-start(f32[4096,256]{0,1:T(8,128)} %convolution_bitcast_fusion) | copy-start | bytes 12582916
Sparse Core Ops, SparseCore 0:
  69.3 127.2 all-reduce.7
  334.5 127.2 all-reduce.5
where the time goes:
time: 565 us; the launch traced here: 554 us
  waiting for transfers between devices  250 us (44%)
  other arithmetic  123 us (22%)
  matrix products  111 us (20%)
  local copies, waits for them, and re-layouts  36.6 us (6%)
  between operations  17.3 us (3%)
  starting transfers between devices  16.3 us (3%)
    psum x2, waiting for transfers between devices, shards(): gram, proj = lax.psum((local_gram, local_proj), ('wide', 'blk'))  242 us
    another operation x13, other arithmetic, shards(): factor = jnp.linalg.cholesky(gram)  68.7 us
    another operation x5, other arithmetic, shards(): alpha = jax.scipy.linalg.cho_solve((factor, True), proj)  39.8 us
    dot_general x8, matrix products, near_apply(): jnp.dot(near_rows[j * NEAR:(j + 1) * NEAR], ext[j * NEAR:j * NEAR + NEAR...  31.3 us
    dot_general x2, matrix products, shards(): residual = residual - jnp.dot(image, alpha, precision=lax.Precision.HIGHEST)  21.2 us
    dot_general x2, matrix products, shards(): jnp.dot(residual, alpha, precision=lax.Precision.HIGHEST)  18 us
    all_to_all x2, starting transfers between devices, shards(): lax.all_to_all(outgoing, ('wide', 'blk'), split_axis=0, concat_axis=0, ti...  13.2 us
    dot_general x2, matrix products, shards(): jnp.einsum('rs,rt->st', image, residual, precision=lax.Precision.HIGHEST)  12.3 us
  transfers between devices with their start and end apart: 8, of which 6 were waited for; matrix products, arithmetic and copies ran while one was open for 9% of the time, Pallas kernels for 0%

commit v1 on v0

--- a/solution.py
+++ b/solution.py
@@ -1,6 +1,10 @@
+import functools
+
 import jax
 import jax.numpy as jnp
 from jax import lax
+from jax.experimental import pallas as pl
+from jax.experimental.pallas import tpu as pltpu
 from jax.sharding import PartitionSpec as P
 
 NEAR = 1024
@@ -33,6 +37,164 @@
             )
         )
     return jnp.concatenate(outs, axis=0)
+
+
+def dot32(a, b):
+    return jnp.dot(a, b, precision=lax.Precision.HIGHEST, preferred_element_type=jnp.float32)
+
+
+def sum_kernel(n, n_blk, part_ref, out_ref, landed, total, sent, got, sent2, got2):
+    me = lax.axis_index("wide") * n_blk + lax.axis_index("blk")
+    chunk = part_ref.shape[0] // n
+
+    def peer_of(d):
+        return lax.rem(me + d, n)
+
+    def place(p):
+        return {"wide": p // n_blk, "blk": lax.rem(p, n_blk)}
+
+    def rows(p):
+        return pl.ds(pl.multiple_of(p * chunk, chunk), chunk)
+
+    barrier = pltpu.get_barrier_semaphore()
+
+    def greet(d, c):
+        pl.semaphore_signal(barrier, inc=1, device_id=place(peer_of(d)), device_id_type=pl.DeviceIdType.MESH)
+        return c
+
+    lax.fori_loop(1, n, greet, 0)
+    pl.semaphore_wait(barrier, n - 1)
+
+    def scatter(d):
+        p = peer_of(d)
+        return pltpu.make_async_remote_copy(
+            src_ref=part_ref.at[rows(p)],
+            dst_ref=landed.at[rows(me)],
+            send_sem=sent.at[d],
+            recv_sem=got.at[me],
+            device_id=place(p),
+            device_id_type=pl.DeviceIdType.MESH,
+        )
+
+    def gather(d):
+        p = peer_of(d)
+        return pltpu.make_async_remote_copy(
+            src_ref=total.at[rows(me)],
+            dst_ref=total.at[rows(me)],
+            send_sem=sent2.at[d],
+            recv_sem=got2.at[me],
+            device_id=place(p),
+            device_id_type=pl.DeviceIdType.MESH,
+        )
+
+    def arrived(ref, sems, d):
+        p = peer_of(d)
+        return pltpu.make_async_remote_copy(
+            src_ref=ref.at[rows(p)],
+            dst_ref=ref.at[rows(p)],
+            send_sem=sent.at[d],
+            recv_sem=sems.at[p],
+            device_id=place(p),
+            device_id_type=pl.DeviceIdType.MESH,
+        )
+
+    def start1(d, c):
+        scatter(d).start()
+        return c
+
+    lax.fori_loop(1, n, start1, 0)
+
+    def add(d, acc):
+        arrived(landed, got, d).wait_recv()
+        return acc + landed[rows(peer_of(d))]
+
+    acc = lax.fori_loop(1, n, add, part_ref[rows(me)])
+    total[rows(me)] = acc
+
+    def start2(d, c):
+        gather(d).start()
+        return c
+
+    lax.fori_loop(1, n, start2, 0)
+
+    def drain(d, c):
+        scatter(d).wait_send()
+        gather(d).wait_send()
+        arrived(total, got2, d).wait_recv()
+        return c
+
+    lax.fori_loop(1, n, drain, 0)
+    out_ref[...] = total[...]
+
+
+def sum_over_devices(part, n, n_blk):
+    return pl.pallas_call(
+        functools.partial(sum_kernel, n, n_blk),
+        out_shape=jax.ShapeDtypeStruct(part.shape, part.dtype),
+        in_specs=[pl.BlockSpec(memory_space=pltpu.VMEM)],
+        out_specs=pl.BlockSpec(memory_space=pltpu.VMEM),
+        scratch_shapes=[
+            pltpu.VMEM(part.shape, part.dtype),
+            pltpu.VMEM(part.shape, part.dtype),
+            pltpu.SemaphoreType.DMA((n,)),
+            pltpu.SemaphoreType.DMA((n,)),
+            pltpu.SemaphoreType.DMA((n,)),
+            pltpu.SemaphoreType.DMA((n,)),
+        ],
+        compiler_params=pltpu.CompilerParams(collective_id=0, has_side_effects=True),
+        name="sum_over_devices",
+    )(part)
+
+
+def inverse(a):
+    size = a.shape[0]
+    lane = lax.broadcasted_iota(jnp.int32, (8, size), 1)
+    sub = lax.broadcasted_iota(jnp.int32, (8, size), 0)
+    wide_lane = lax.broadcasted_iota(jnp.int32, (size - 8, size), 1)
+
+    def step(_, a):
+        top, rest = a[:8], a[8:]
+        cols = [jnp.broadcast_to(top[:, i : i + 1], top.shape) for i in range(8)]
+        for i in range(8):
+            col = cols[i]
+            inv = 1.0 / col[i : i + 1]
+            row = jnp.where(lane[:1] == i, inv, top[i : i + 1] * inv)
+            top = jnp.where(sub == i, row, jnp.where(lane == i, 0.0, top) - col * row)
+            for m in range(i + 1, 8):
+                t = cols[m][i : i + 1] * inv
+                cols[m] = jnp.where(sub == i, t, cols[m] - col * t)
+        new = jnp.where(wide_lane < 8, 0.0, rest)
+        for i in range(8):
+            new = new - rest[:, i : i + 1] * top[i : i + 1]
+        return pltpu.roll(jnp.concatenate([new, top], axis=0), size - 8, 1)
+
+    return lax.fori_loop(0, size // 8, step, a)
+
+
+def solve_kernel(both_ref, alpha_ref):
+    width = both_ref.shape[1]
+    full = 2 * width
+    g11, g21 = both_ref[:width], both_ref[width:full]
+    g12, g22 = both_ref[full : full + width], both_ref[full + width : 2 * full]
+    p1 = jnp.concatenate([both_ref[2 * full : 2 * full + width], both_ref[3 * full : 3 * full + width]], axis=1)
+    p2 = jnp.concatenate([both_ref[2 * full + width : 3 * full], both_ref[3 * full + width :]], axis=1)
+    inv1 = inverse(g11)
+    across = dot32(inv1, g12)
+    part1 = dot32(inv1, p1)
+    inv2 = inverse(g22 - dot32(g21, across))
+    part2 = dot32(inv2, p2 - dot32(g21, part1))
+    alpha_ref[width:] = part2
+    alpha_ref[:width] = part1 - dot32(across, part2)
+
+
+def solve(both, width):
+    return pl.pallas_call(
+        solve_kernel,
+        out_shape=jax.ShapeDtypeStruct((width, width), jnp.float32),
+        in_specs=[pl.BlockSpec(memory_space=pltpu.VMEM)],
+        out_specs=pl.BlockSpec(memory_space=pltpu.VMEM),
+        name="solve",
+    )(both)
 
 
 def shards(rhs, near_blocks, source_basis, target_basis, far_coupling, send_ids, far_list):
@@ -70,9 +232,13 @@
         image = residual + near + far
         local_gram = jnp.einsum("rs,rt->st", image, image, precision=lax.Precision.HIGHEST)
         local_proj = jnp.einsum("rs,rt->st", image, residual, precision=lax.Precision.HIGHEST)
-        gram, proj = lax.psum((local_gram, local_proj), ("wide", "blk"))
-        factor = jnp.linalg.cholesky(gram)
-        alpha = jax.scipy.linalg.cho_solve((factor, True), proj)
+        half = width // 2
+        part = jnp.concatenate(
+            [local_gram[:, :half], local_gram[:, half:], local_proj[:, :half], local_proj[:, half:]], axis=0
+        )
+        n_blk = lax.axis_size("blk")
+        both = sum_over_devices(part, lax.axis_size("wide") * n_blk, n_blk)
+        alpha = solve(both, width)
         solution = solution + jnp.dot(residual, alpha, precision=lax.Precision.HIGHEST)
         residual = residual - jnp.dot(image, alpha, precision=lax.Precision.HIGHEST)
     return (solution, residual)

time: 565 us -> 255 us (0.45); the launches traced: 554 us -> 251 us
  waiting for transfers between devices: 250 us -> 2.38 us
  other arithmetic: 123 us -> 14.3 us
  Pallas kernels: 0 us -> 95.7 us
  matrix products: 111 us -> 94.4 us
  between operations: 17.3 us -> 1.13 us
  local copies, waits for them, and re-layouts: 36.6 us -> 27.9 us
    psum x2 -> x0, waiting for transfers between devices: 242 us -> none  [shards(): gram, proj = lax.psum((local_gram, local_proj), ('wide', 'blk'))]
    another operation x18 -> x0, other arithmetic: 109 us -> none  [the longest x13 68.7 us: shards(): factor = jnp.linalg.cholesky(gram)]
    pallas_call x0 -> x4, Pallas kernels: none -> 95.7 us  [the longest x2 70.5 us: sum_over_devices(): pl.pallas_call(functools.partial(sum_kernel, n, n_blk), out_shape=jax.Sha...]
    another operation x19 -> x0, local copies, waits for them, and re-layouts: 7.94 us -> none  [the longest x15 7.89 us: shards(): alpha = jax.scipy.linalg.cho_solve((factor, True), proj)]
    another operation x16 -> x0, matrix products: 6.16 us -> none  [the longest x12 5.22 us: shards(): alpha = jax.scipy.linalg.cho_solve((factor, True), proj)]
    unnamed x34 -> x40, local copies, waits for them, and re-layouts: 11.3 us -> 12.7 us
  transfers between devices with their start and end apart: 8 -> 6, of which waited for: 6 -> 3; matrix products, arithmetic and copies ran while one was open for 9% -> 17% of each run, Pallas kernels for 0% -> 0%
where the time goes in v1:
time: 255 us; the launch traced here: 251 us
  Pallas kernels  95.7 us (38%)
  matrix products  94.4 us (37%)
  local copies, waits for them, and re-layouts  27.9 us (11%)
  starting transfers between devices  15.1 us (6%)
  other arithmetic  14.3 us (6%)
    pallas_call x2, Pallas kernels, sum_over_devices(): pl.pallas_call(functools.partial(sum_kernel, n, n_blk), out_shape=jax.Sha...  70.5 us
    dot_general x8, matrix products, near_apply(): jnp.dot(near_rows[j * NEAR:(j + 1) * NEAR], ext[j * NEAR:j * NEAR + NEAR...  27.9 us
    pallas_call x2, Pallas kernels, solve(): pl.pallas_call(solve_kernel, out_shape=jax.ShapeDtypeStruct((width, width...  25.2 us
    dot_general x2, matrix products, shards(): residual = residual - jnp.dot(image, alpha, precision=lax.Precision.HIGHEST)  21.3 us
    dot_general x2, matrix products, shards(): jnp.dot(residual, alpha, precision=lax.Precision.HIGHEST)  13.9 us
    unnamed x40, local copies, waits for them, and re-layouts  12.7 us
    all_to_all x2, starting transfers between devices, shards(): lax.all_to_all(outgoing, ('wide', 'blk'), split_axis=0, concat_axis=0, ti...  11.8 us
    dot_general x2, matrix products, shards(): jnp.einsum('rs,rt->st', image, image, precision=lax.Precision.HIGHEST)  10.8 us
  transfers between devices with their start and end apart: 6, of which 3 were waited for; matrix products, arithmetic and copies ran while one was open for 17% of the time, Pallas kernels for 0%

profile of v1, /device:TPU:29, one launch (start us, length us, event | category | flops | bytes accessed | tf_op | source)
XLA Modules:
  0.0 250.9 jit_solution(16991587308277712905)
XLA Ops:
  0.6 0.0 copy-start
  0.6 0.0 copy-start.10
  0.7 0.7 fusion.59
  1.4 2.4 convert_element_type.23
  3.8 0.0 copy-done.10
  3.8 1.4 convolution_convert_fusion.1
  5.2 2.8 %gather_fusion = bf16[32,64,256]{2,1,0:T(8,128)(2,1)} fusion(bf16[32,64,256]{2,1,0:T(8,128)(2,1)} %convolution_convert_fusion.1, s32[1024]{0:T(1024)S(1)} %pad_clamp_fusion.1), kind=kCustom, calls=%fused_computation | custom fusion | bytes 2097280 | tf_op jit(solution)/shard_map/gather | solution.py:220
  8.0 6.2 %all-to-all-start = ((bf16[32,64,256]{2,1,0:T(8,128)(2,1)}), bf16[32,64,256]{2,1,0:T(8,128)(2,1)}, u32[]{:S(2)}, u32[]{:S(2)}) async-start(bf16[32,64,256]{2,1,0:T(8,128)(2,1)} %gather_fusion), calls=%async_computation | async-start | bytes 2097152 | tf_op jit(solution)/shard_map/all_to_all | solution.py:221
  14.2 1.5 collective-permute-start
  15.8 0.0 collective-permute-start.1
  15.8 3.9 %fusion.8 = f32[1024,256]{0,1:T(8,128)} fusion(bf16[4096,1536]{1,0:T(8,128)(2,1)} %param.8, bf16[4096,256]{1,0:T(8,128)(2,1)S(1)} %convert_element_type.23), kind=kOutput, calls=%fused_computation.18 | convolution fusion | flops 805306368 | bytes 4980736 | tf_op jit(solution)/shard_map/dot_general | solution.py:33
  19.7 4.0 %fusion.12 = f32[1024,256]{0,1:T(8,128)} fusion(bf16[4096,1536]{1,0:T(8,128)(2,1)} %param.8, bf16[4096,256]{1,0:T(8,128)(2,1)S(1)} %convert_element_type.23), kind=kOutput, calls=%fused_computation.22 | convolution fusion | flops 805306368 | bytes 4980736 | tf_op jit(solution)/shard_map/dot_general | solution.py:33
  23.7 0.0 copy-done.15
  23.7 5.8 %copy.35 = f32[4096,256]{0,1:T(8,128)} copy(f32[4096,256]{1,0:T(8,128)} %param.7) | data formatting | bytes 8388608 | tf_op args[0]
  29.5 0.0 collective-permute-done.1
  29.5 4.0 %fusion.33 = f32[1024,256]{0,1:T(8,128)} fusion(bf16[4096,1536]{1,0:T(8,128)(2,1)} %param.8, bf16[256,256]{1,0:T(8,128)(2,1)} %collective-permute-done.1, bf16[4096,256]{1,0:T(8,128)(2,1)S(1)} %convert_element_type.23), kind=kOutput, calls=%fused_computation.39 | convolution fusion | flops 806879232 | bytes 6422528 | tf_op jit(solution)/shard_map/dot_general | solution.py:33
  33.5 0.0 collective-permute-done
  33.5 4.0 %fusion.21 = f32[1024,256]{0,1:T(8,128)} fusion(bf16[4096,1536]{1,0:T(8,128)(2,1)} %param.8, bf16[4096,256]{1,0:T(8,128)(2,1)S(1)} %convert_element_type.23, bf16[256,256]{1,0:T(8,128)(2,1)S(1)} %collective-permute-done), kind=kOutput, calls=%fused_computation.35 | convolution fusion | flops 806879232 | bytes 6422528 | tf_op jit(solution)/shard_map/dot_general | solution.py:33
  37.4 0.8 all-to-all-done
  38.2 1.8 gather_fusion.1
  40.1 0.0 copy-done
  40.1 4.0 %fusion.19 = f32[32,256,128]{1,2,0:T(8,128)} fusion(bf16[32,64,256]{2,1,0:T(8,128)(2,1)S(1)} %gather_fusion.1, bf16[32,1,64,64]{3,2,1,0:T(8,128)(2,1)S(1)} %copy-done, bf16[4096,64]{0,1:T(8,128)(2,1)} %param.10), kind=kOutput, calls=%fused_computation.33 | convolution fusion | flops 201850880 | bytes 6029312 | tf_op jit(solution)/shard_map/lia,las->lis/dot_general | solution.py:229
  44.1 5.7 %copy.54 = f32[4096,256]{0,1:T(8,128)} copy(f32[4096,256]{1,0:T(8,128)} %bitcast.84) | data formatting | bytes 8388608 | tf_op jit(solution)/shard_map/reshape | solution.py:231
  49.8 0.0 copy-done.13
  49.8 0.0 copy-done.14
  49.8 4.5 %fusion = f32[4096,256]{0,1:T(8,128)S(1)} fusion(f32[4096,256]{0,1:T(8,128)} %copy.54, f32[4096,256]{0,1:T(8,128)} %copy.35, f32[1024,256]{0,1:T(8,128)} %fusion.33, f32[1024,256]{0,1:T(8,128)S(1)} %copy-done.13, f32[1024,256]{0,1:T(8,128)S(1)} %copy-done.14, f32[1024,256]{0,1:T(8,128)} %fusion.21), kind=kLoop, calls=%fused_computation.9 | loop fusion | flops 5242880 | bytes 16777216 | tf_op jit(solution)/shard_map/add | solution.py:232
  54.3 0.8 copy-done.1
  55.1 3.6 %fusion.73 = f32[256,256]{1,0:T(8,128)S(1)} fusion(f32[4096,256]{0,1:T(8,128)S(1)} %fusion, f32[4096,256]{1,0:T(8,128)S(1)} %copy-done.1), kind=kOutput, calls=%fused_computation.83 | convolution fusion | flops 3221225472 | bytes 8650752 | tf_op jit(solution)/shard_map/rs,rt->st/dot_general | solution.py:234
  58.7 3.5 %fusion.72 = f32[256,256]{1,0:T(8,128)S(1)} fusion(f32[4096,256]{0,1:T(8,128)S(1)} %fusion), kind=kOutput, calls=%fused_computation.82 | convolution fusion | flops 3221225472 | bytes 4456448 | tf_op jit(solution)/shard_map/rs,rt->st/dot_general | solution.py:233
  62.3 0.8 pad_maximum_fusion.8.part_ref
  63.1 35.2 %sum_over_devices.2.both_ref = f32[1024,128]{1,0:T(8,128)} custom-call(f32[1024,128]{1,0:T(8,128)} %pad_maximum_fusion.8.part_ref), custom_call_target="tpu_custom_call" | custom-call | tf_op jit(solution)/shard_map/sum_over_devices/pallas_call | solution.py:131
  98.3 12.8 %solve.2 = f32[256,256]{1,0:T(8,128)} custom-call(f32[1024,128]{1,0:T(8,128)} %sum_over_devices.2.both_ref), custom_call_target="tpu_custom_call" | custom-call | tf_op jit(solution)/shard_map/solve/pallas_call | solution.py:191
  111.1 12.2 %fusion.71 = (bf16[4096,256]{1,0:T(8,128)(2,1)S(1)}, f32[4096,256]{1,0:T(8,128)}) fusion(f32[4096,256]{1,0:T(8,128)} %param.7, f32[4096,256]{0,1:T(8,128)} %copy-done.5, f32[256,256]{1,0:T(8,128)} %solve.2), kind=kOutput, calls=%fused_computation.81 | convolution fusion | flops 3223322624 | bytes 14942208 | tf_op jit(solution)/shard_map/dot_general | solution.py:243
  123.3 1.4 fusion.18
  124.7 2.8 %gather_fusion.2 = bf16[32,64,256]{2,1,0:T(8,128)(2,1)} fusion(bf16[32,64,256]{2,1,0:T(8,128)(2,1)} %fusion.18, s32[1024]{0:T(1024)S(1)} %pad_clamp_fusion.1), kind=kCustom, calls=%fused_computation.2 | custom fusion | bytes 2097280 | tf_op jit(solution)/shard_map/gather | solution.py:220
  127.5 5.6 %all-to-all-start.1 = ((bf16[32,64,256]{2,1,0:T(8,128)(2,1)}), bf16[32,64,256]{2,1,0:T(8,128)(2,1)}, u32[]{:S(2)}, u32[]{:S(2)}) async-start(bf16[32,64,256]{2,1,0:T(8,128)(2,1)} %gather_fusion.2), calls=%async_computation.1 | async-start | bytes 2097152 | tf_op jit(solution)/shard_map/all_to_all | solution.py:221
  133.2 0.0 copy-start.2
  133.2 0.0 copy-start.8
  133.2 0.4 collective-permute-start.3
  133.7 4.1 %fusion.30 = f32[1024,256]{1,0:T(8,128)} fusion(bf16[4096,1536]{1,0:T(8,128)(2,1)} %param.8, bf16[4096,256]{1,0:T(8,128)(2,1)S(1)} %get-tuple-element.20), kind=kOutput, calls=%fused_computation.38 | convolution fusion | flops 805306368 | bytes 4980736 | tf_op jit(solution)/shard_map/dot_general | solution.py:33
  137.8 8.5 %convolution_bitcast_fusion = f32[4096,256]{0,1:T(8,128)} fusion(f32[256,256]{1,0:T(8,128)S(1)} %copy-done.8, f32[4096,256]{1,0:T(8,128)S(1)} %copy-done.2), kind=kOutput, calls=%fused_computation.7 | convolution fusion | flops 3221225472 | bytes 8650752 | tf_op jit(solution)/shard_map/dot_general | solution.py:242
  146.2 4.1 %fusion.27 = f32[1024,256]{1,0:T(8,128)} fusion(bf16[4096,1536]{1,0:T(8,128)(2,1)} %param.8, bf16[4096,256]{1,0:T(8,128)(2,1)S(1)} %get-tuple-element.20), kind=kOutput, calls=%fused_computation.37 | convolution fusion | flops 805306368 | bytes 4980736 | tf_op jit(solution)/shard_map/dot_general | solution.py:33
  150.3 1.3 collective-permute-start.2
  151.6 0.0 collective-permute-done.3
  151.6 0.0 slice-done.1
  151.6 2.0 fusion.36
  153.6 1.0 collective-permute-done.2
  154.6 2.0 fusion.24
  156.6 0.6 all-to-all-done.1
  157.2 1.8 gather_fusion.3
  159.0 0.0 copy-done.11
  159.0 3.0 %fusion.20 = f32[32,256,128]{1,2,0:T(8,128)} fusion(bf16[32,64,256]{2,1,0:T(8,128)(2,1)S(1)} %gather_fusion.3, bf16[32,1,64,64]{3,2,1,0:T(8,128)(2,1)S(1)} %copy-done, bf16[4096,64]{0,1:T(8,128)(2,1)S(1)} %copy-done.11), kind=kOutput, calls=%fused_computation.34 | convolution fusion | flops 201850880 | bytes 6029312 | tf_op jit(solution)/shard_map/lia,las->lis/dot_general | solution.py:229
  162.0 0.0 copy-done.12
  162.0 5.0 %fusion.1 = f32[4096,256]{1,0:T(8,128)S(1)} fusion(f32[4096,256]{1,0:T(8,128)} %get-tuple-element.21, f32[1024,256]{1,0:T(8,128)} %fusion.36, f32[1024,256]{1,0:T(8,128)S(1)} %copy-done.12, f32[1024,256]{1,0:T(8,128)} %fusion.27, f32[1024,256]{1,0:T(8,128)} %fusion.24, f32[32,256,128]{1,2,0:T(8,128)} %fusion.20), kind=kLoop, calls=%fused_computation.11 | loop fusion | flops 5242880 | bytes 16777216 | tf_op jit(solution)/shard_map/add | solution.py:232
  167.1 0.5 copy-done.3
  167.6 7.0 %fusion.75 = f32[256,256]{1,0:T(8,128)S(1)} fusion(f32[4096,256]{1,0:T(8,128)S(1)} %fusion.1, f32[4096,256]{1,0:T(8,128)S(1)} %copy-done.3), kind=kOutput, calls=%fused_computation.85 | convolution fusion | flops 3221225472 | bytes 8650752 | tf_op jit(solution)/shard_map/rs,rt->st/dot_general | solution.py:234
  174.6 0.0 copy-done.6
  174.6 7.3 %fusion.74 = f32[256,256]{1,0:T(8,128)S(1)} fusion(f32[4096,256]{1,0:T(8,128)S(1)} %fusion.1), kind=kOutput, calls=%fused_computation.84 | convolution fusion | flops 3221225472 | bytes 4456448 | tf_op jit(solution)/shard_map/rs,rt->st/dot_general | solution.py:233
  181.9 0.8 pad_maximum_fusion.9.part_ref
  182.8 35.3 %sum_over_devices.3.both_ref = f32[1024,128]{1,0:T(8,128)} custom-call(f32[1024,128]{1,0:T(8,128)} %pad_maximum_fusion.9.part_ref), custom_call_target="tpu_custom_call" | custom-call | tf_op jit(solution)/shard_map/sum_over_devices/pallas_call | solution.py:131
  218.1 12.4 %solve.3 = f32[256,256]{1,0:T(8,128)} custom-call(f32[1024,128]{1,0:T(8,128)} %sum_over_devices.3.both_ref), custom_call_target="tpu_custom_call" | custom-call | tf_op jit(solution)/shard_map/solve/pallas_call | solution.py:191
  230.5 9.1 %convolution_subtract_fusion = f32[4096,256]{1,0:T(8,128)} fusion(f32[4096,256]{1,0:T(8,128)} %get-tuple-element.21, f32[4096,256]{1,0:T(8,128)} %copy-done.6, f32[256,256]{1,0:T(8,128)} %solve.3), kind=kOutput, calls=%fused_computation.4 | convolution fusion | flops 3222274048 | bytes 12845056 | tf_op jit(solution)/shard_map/dot_general | solution.py:243
  239.6 5.4 %convolution_add_fusion = f32[4096,256]{0,1:T(8,128)} fusion(f32[4096,256]{0,1:T(8,128)S(1)} %copy-done.7, f32[4096,256]{1,0:T(8,128)S(1)} %copy-done.4, f32[256,256]{1,0:T(8,128)S(1)} %copy-done.9), kind=kOutput, calls=%fused_computation.5 | convolution fusion | flops 3222274048 | bytes 12845056 | tf_op jit(solution)/shard_map/dot_general | solution.py:242
  245.0 5.6 %copy.46 = f32[4096,256]{1,0:T(8,128)} copy(f32[4096,256]{0,1:T(8,128)} %convolution_add_fusion) | data formatting | bytes 8388608
  (32 shorter events, 0.2 us)
Async XLA Ops:
  0.6 39.4 %copy-start = (bf16[32,1,64,64]{3,2,1,0:T(8,128)(2,1)S(1)}, bf16[32,1,64,64]{3,2,1,0:T(8,128)(2,1)}, u32[]{:S(2)}) copy-start(bf16[32,1,64,64]{3,2,1,0:T(8,128)(2,1)} %param.11) | copy-start | bytes 786436
  0.6 3.2 %copy-start.10 = (bf16[4096,64]{0,1:T(8,128)(2,1)S(1)}, bf16[4096,64]{0,1:T(8,128)(2,1)}, u32[]{:S(2)}) copy-start(bf16[4096,64]{0,1:T(8,128)(2,1)} %param.9) | copy-start | bytes 1572868
  8.0 30.2 %all-to-all-start = ((bf16[32,64,256]{2,1,0:T(8,128)(2,1)}), bf16[32,64,256]{2,1,0:T(8,128)(2,1)}, u32[]{:S(2)}, u32[]{:S(2)}) async-start(bf16[32,64,256]{2,1,0:T(8,128)(2,1)} %gather_fusion), calls=%async_computation | async-start | bytes 2097152 | tf_op jit(solution)/shard_map/all_to_all | solution.py:221
  14.2 19.2 %collective-permute-start = (bf16[256,256]{1,0:T(8,128)(2,1)S(1)}, bf16[256,256]{1,0:T(8,128)(2,1)S(1)}, u32[]{:S(2)}, u32[]{:S(2)}) collective-permute-start(bf16[256,256]{1,0:T(8,128)(2,1)S(1)} %get-tuple-element.10), channel_id=1, source_target_pairs={{0,1},{1,2},{2,3},{3,4},{4,5},{5,6},{6,7},{7,0},{8,9},{9,10},{10,1... | collective-permute-start | bytes 393224 | tf_op jit(solution)/shard_map/ppermute | solution.py:23
  15.8 13.7 %collective-permute-start.1 = (bf16[256,256]{1,0:T(8,128)(2,1)S(1)}, bf16[256,256]{1,0:T(8,128)(2,1)}, u32[]{:S(2)}, u32[]{:S(2)}) collective-permute-start(bf16[256,256]{1,0:T(8,128)(2,1)S(1)} %get-tuple-element.11), channel_id=1, source_target_pairs={{1,0},{2,1},{3,2},{4,3},{5,4},{6,5},{7,6},{0,7},{9,8},{10,9},{11,1... | collective-permute-start | bytes 393224 | tf_op jit(solution)/shard_map/ppermute | solution.py:24
  19.7 4.0 %copy-start.15 = (s32[1,32]{1,0:T(1,128)S(1)}, s32[1,32]{1,0:T(1,128)}, u32[]{:S(2)}) copy-start(s32[1,32]{1,0:T(1,128)} %param.13) | copy-start | bytes 388
  44.1 5.7 %copy-start.13 = (f32[1024,256]{0,1:T(8,128)S(1)}, f32[1024,256]{0,1:T(8,128)}, u32[]{:S(2)}) copy-start(f32[1024,256]{0,1:T(8,128)} %fusion.8) | copy-start | bytes 3145732
  44.1 5.7 %copy-start.14 = (f32[1024,256]{0,1:T(8,128)S(1)}, f32[1024,256]{0,1:T(8,128)}, u32[]{:S(2)}) copy-start(f32[1024,256]{0,1:T(8,128)} %fusion.12) | copy-start | bytes 3145732
  49.8 5.3 %copy-start.1 = (f32[4096,256]{1,0:T(8,128)S(1)}, f32[4096,256]{1,0:T(8,128)}, u32[]{:S(2)}) copy-start(f32[4096,256]{1,0:T(8,128)} %param.7) | copy-start | bytes 12582916
  55.1 3.6 %copy-start.5 = (f32[4096,256]{0,1:T(8,128)}, f32[4096,256]{0,1:T(8,128)S(1)}, u32[]{:S(2)}) copy-start(f32[4096,256]{0,1:T(8,128)S(1)} %fusion) | copy-start | bytes 12582916
  127.5 29.6 %all-to-all-start.1 = ((bf16[32,64,256]{2,1,0:T(8,128)(2,1)}), bf16[32,64,256]{2,1,0:T(8,128)(2,1)}, u32[]{:S(2)}, u32[]{:S(2)}) async-start(bf16[32,64,256]{2,1,0:T(8,128)(2,1)} %gather_fusion.2), calls=%async_computation.1 | async-start | bytes 2097152 | tf_op jit(solution)/shard_map/all_to_all | solution.py:221
  133.2 4.5 %copy-start.2 = (f32[4096,256]{1,0:T(8,128)S(1)}, f32[4096,256]{1,0:T(8,128)}, u32[]{:S(2)}) copy-start(f32[4096,256]{1,0:T(8,128)} %param.7) | copy-start | bytes 12582916
  133.2 4.5 %copy-start.8 = (f32[256,256]{1,0:T(8,128)S(1)}, f32[256,256]{1,0:T(8,128)}, u32[]{:S(2)}) copy-start(f32[256,256]{1,0:T(8,128)} %solve.2) | copy-start | bytes 786436
  133.2 18.4 %collective-permute-start.3 = (bf16[256,256]{1,0:T(8,128)(2,1)S(1)}, bf16[256,256]{1,0:T(8,128)(2,1)S(1)}, u32[]{:S(2)}, u32[]{:S(2)}) collective-permute-start(bf16[256,256]{1,0:T(8,128)(2,1)S(1)} %get-tuple-element.9), channel_id=1, source_target_pairs={{1,0},{2,1},{3,2},{4,3},{5,4},{6,5},{7,6},{0,7},{9,8},{10,9},{11,1... | collective-permute-start | bytes 393224 | tf_op jit(solution)/shard_map/ppermute | solution.py:24
  133.7 17.9 %slice-start = ((s8[12582912]{0:T(1024)(128)(4,1)}), s8[4194304]{0:T(1024)(128)(4,1)S(1)}, s32[]{:S(2)}) async-start(s8[12582912]{0:T(1024)(128)(4,1)} %bitcast.87), calls=%async_computation.2 | async-start | bytes 8388608
  133.7 17.9 %slice-start.1 = ((s8[12582912]{0:T(1024)(128)(4,1)}), s8[4194304]{0:T(1024)(128)(4,1)S(1)}, s32[]{:S(2)}) async-start(s8[12582912]{0:T(1024)(128)(4,1)} %bitcast.87), calls=%async_computation.3 | async-start | bytes 8388608
  146.2 5.4 %slice-start.2 = ((s8[12582912]{0:T(1024)(128)(4,1)}), s8[4194304]{0:T(1024)(128)(4,1)S(1)}, s32[]{:S(2)}) async-start(s8[12582912]{0:T(1024)(128)(4,1)} %bitcast.87), calls=%async_computation.4 | async-start | bytes 8388608
  150.3 4.3 %collective-permute-start.2 = (bf16[256,256]{1,0:T(8,128)(2,1)S(1)}, bf16[256,256]{1,0:T(8,128)(2,1)S(1)}, u32[]{:S(2)}, u32[]{:S(2)}) collective-permute-start(bf16[256,256]{1,0:T(8,128)(2,1)S(1)} %get-tuple-element.8), channel_id=1, source_target_pairs={{0,1},{1,2},{2,3},{3,4},{4,5},{5,6},{6,7},{7,0},{8,9},{9,10},{10,1... | collective-permute-start | bytes 393224 | tf_op jit(solution)/shard_map/ppermute | solution.py:23
  153.6 5.4 %copy-start.11 = (bf16[4096,64]{0,1:T(8,128)(2,1)S(1)}, bf16[4096,64]{0,1:T(8,128)(2,1)}, u32[]{:S(2)}) copy-start(bf16[4096,64]{0,1:T(8,128)(2,1)} %param.10) | copy-start | bytes 1572868
  156.6 5.5 %copy-start.12 = (f32[1024,256]{1,0:T(8,128)S(1)}, f32[1024,256]{1,0:T(8,128)}, u32[]{:S(2)}) copy-start(f32[1024,256]{1,0:T(8,128)} %fusion.30) | copy-start | bytes 3145732
  162.0 5.5 %copy-start.3 = (f32[4096,256]{1,0:T(8,128)S(1)}, f32[4096,256]{1,0:T(8,128)}, u32[]{:S(2)}) copy-start(f32[4096,256]{1,0:T(8,128)} %get-tuple-element.21) | copy-start | bytes 12582916
  167.6 7.0 %copy-start.6 = (f32[4096,256]{1,0:T(8,128)}, f32[4096,256]{1,0:T(8,128)S(1)}, u32[]{:S(2)}) copy-start(f32[4096,256]{1,0:T(8,128)S(1)} %fusion.1) | copy-start | bytes 12582916
  230.5 9.1 %copy-start.4 = (f32[4096,256]{1,0:T(8,128)S(1)}, f32[4096,256]{1,0:T(8,128)}, u32[]{:S(2)}) copy-start(f32[4096,256]{1,0:T(8,128)} %get-tuple-element.21) | copy-start | bytes 12582916
  230.5 9.1 %copy-start.7 = (f32[4096,256]{0,1:T(8,128)S(1)}, f32[4096,256]{0,1:T(8,128)}, u32[]{:S(2)}) copy-start(f32[4096,256]{0,1:T(8,128)} %convolution_bitcast_fusion) | copy-start | bytes 12582916
  230.5 9.1 %copy-start.9 = (f32[256,256]{1,0:T(8,128)S(1)}, f32[256,256]{1,0:T(8,128)}, u32[]{:S(2)}) copy-start(f32[256,256]{1,0:T(8,128)} %solve.3) | copy-start | bytes 786436

commit v2 on v1

--- a/solution.py
+++ b/solution.py
@@ -13,30 +13,11 @@
 ITERS = 2
 
 
-def with_halo(value, sides, width):
-    for axis, dim in sides:
-        count, length = (lax.axis_size(axis), value.shape[dim])
-        up = [(i, (i + 1) % count) for i in range(count)]
-        down = [(j, i) for i, j in up]
-        last = lax.slice_in_dim(value, length - width, length, axis=dim)
-        first = lax.slice_in_dim(value, 0, width, axis=dim)
-        before = lax.ppermute(last, axis, up)
-        after = lax.ppermute(first, axis, down)
-        value = jnp.concatenate([before, value, after], axis=dim)
-    return value
-
-
-def near_apply(near_rows, ext):
-    outs = []
-    for j in range(near_rows.shape[0] // NEAR):
-        outs.append(
-            jnp.dot(
-                near_rows[j * NEAR : (j + 1) * NEAR],
-                ext[j * NEAR : j * NEAR + NEAR + 2 * HALO],
-                preferred_element_type=jnp.float32,
-            )
-        )
-    return jnp.concatenate(outs, axis=0)
+def sides(value, axis, width):
+    count, length = lax.axis_size(axis), value.shape[0]
+    up = [(i, (i + 1) % count) for i in range(count)]
+    down = [(j, i) for i, j in up]
+    return lax.ppermute(value[length - width :], axis, up), lax.ppermute(value[:width], axis, down)
 
 
 def dot32(a, b):
@@ -197,20 +178,181 @@
     )(both)
 
 
+TILE = 512
+WHOLE = pl.BlockSpec(memory_space=pltpu.VMEM)
+
+
+def split(x):
+    high = x.astype(jnp.bfloat16)
+    return high, (x - high.astype(jnp.float32)).astype(jnp.bfloat16)
+
+
+def dot16(a, b):
+    return jnp.dot(a, b, preferred_element_type=jnp.float32)
+
+
+def tdot16(a, b):
+    return lax.dot_general(a, b, (((0,), (0,)), ((), ())), preferred_element_type=jnp.float32)
+
+
+def tiles(width):
+    return pl.BlockSpec((TILE, width), lambda i: (i, 0))
+
+
+def near_kernel(near_ref, vb_ref, before_ref, after_ref, res_ref, out_ref, ext):
+    i = pl.program_id(0)
+    halo, rows = before_ref.shape[0], vb_ref.shape[0]
+
+    @pl.when(i == 0)
+    def _():
+        ext[:halo] = before_ref[...]
+        ext[halo : halo + rows] = vb_ref[...]
+        ext[halo + rows :] = after_ref[...]
+
+    start = pl.multiple_of((i * TILE) // NEAR * NEAR, NEAR)
+    out_ref[...] = res_ref[...] + dot16(near_ref[...], ext[pl.ds(start, near_ref.shape[1])])
+
+
+def near_base(near_blocks, vb, before, after, residual):
+    rows, width = residual.shape
+    return pl.pallas_call(
+        near_kernel,
+        grid=(rows // TILE,),
+        out_shape=jax.ShapeDtypeStruct(residual.shape, jnp.float32),
+        in_specs=[tiles(near_blocks.shape[1]), WHOLE, WHOLE, WHOLE, tiles(width)],
+        out_specs=tiles(width),
+        scratch_shapes=[pltpu.VMEM((rows + 2 * HALO, width), jnp.bfloat16)],
+        cost_estimate=pl.CostEstimate(
+            flops=2 * rows * near_blocks.shape[1] * width, bytes_accessed=2 * near_blocks.size + 8 * residual.size, transcendentals=0
+        ),
+        name="near",
+    )(near_blocks, vb, before, after, residual)
+
+
+def image_kernel(fanout, list_ref, base_ref, res_ref, incoming_ref, coupling_ref, target_ref, image_ref, part_ref, cross):
+    i = pl.program_id(0)
+    width = base_ref.shape[1]
+    half = width // 2
+    leaves = TILE // LEAF
+
+    @pl.when(i == 0)
+    def _():
+        part_ref[...] = jnp.zeros_like(part_ref)
+        cross[...] = jnp.zeros_like(cross)
+
+    for l in range(leaves):
+        trans = 0.0
+        for f in range(fanout):
+            trans = trans + dot16(coupling_ref[l, f], incoming_ref[list_ref[(i * leaves + l) * fanout + f]])
+        far = tdot16(target_ref[:, l * LEAF : (l + 1) * LEAF], trans.astype(jnp.bfloat16))
+        image_ref[l * LEAF : (l + 1) * LEAF] = base_ref[l * LEAF : (l + 1) * LEAF] + far
+    high, low = split(image_ref[...])
+    res_high, res_low = split(res_ref[...])
+    gram = tdot16(high, high)
+    proj = tdot16(high, res_high) + tdot16(high, res_low) + tdot16(low, res_high)
+    cross[...] += tdot16(high, low)
+    part_ref[:width] += gram[:, :half]
+    part_ref[width : 2 * width] += gram[:, half:]
+    part_ref[2 * width : 3 * width] += proj[:, :half]
+    part_ref[3 * width :] += proj[:, half:]
+
+    @pl.when(i == pl.num_programs(0) - 1)
+    def _():
+        both = cross[...] + cross[...].T
+        part_ref[:width] += both[:, :half]
+        part_ref[width : 2 * width] += both[:, half:]
+
+
+def image_and_sums(readers, base, residual, incoming, coupling, target_t):
+    rows, width = residual.shape
+    leaves, fanout, rank, _ = coupling.shape
+    step = TILE // LEAF
+    return pl.pallas_call(
+        functools.partial(image_kernel, fanout),
+        grid=(rows // TILE,),
+        out_shape=(
+            jax.ShapeDtypeStruct(residual.shape, jnp.float32),
+            jax.ShapeDtypeStruct((4 * width, width // 2), jnp.float32),
+        ),
+        in_specs=[
+            pl.BlockSpec(memory_space=pltpu.SMEM),
+            tiles(width),
+            tiles(width),
+            WHOLE,
+            pl.BlockSpec((step, fanout, rank, rank), lambda i: (i, 0, 0, 0)),
+            pl.BlockSpec((rank, TILE), lambda i: (0, i)),
+        ],
+        out_specs=(tiles(width), pl.BlockSpec((4 * width, width // 2), lambda i: (0, 0))),
+        scratch_shapes=[pltpu.VMEM((width, width), jnp.float32)],
+        name="image",
+    )(readers, base, residual, incoming, coupling, target_t)
+
+
+def product(x, alpha_ref):
+    high, low = split(x)
+    a_high, a_low = split(alpha_ref[...])
+    return dot16(high, a_high) + dot16(high, a_low) + dot16(low, a_high)
+
+
+def update_kernel(res_ref, image_ref, alpha_ref, new_ref, vb_ref):
+    new = res_ref[...] - product(image_ref[...], alpha_ref)
+    new_ref[...] = new
+    vb_ref[...] = new.astype(jnp.bfloat16)
+
+
+def update(residual, image, alpha):
+    rows, width = residual.shape
+    return pl.pallas_call(
+        update_kernel,
+        grid=(rows // TILE,),
+        out_shape=(
+            jax.ShapeDtypeStruct(residual.shape, jnp.float32),
+            jax.ShapeDtypeStruct(residual.shape, jnp.bfloat16),
+        ),
+        in_specs=[tiles(width), tiles(width), WHOLE],
+        out_specs=(tiles(width), tiles(width)),
+        name="update",
+    )(residual, image, alpha)
+
+
+def last_kernel(count, *refs):
+    residuals, alphas, image_ref = refs[:count], refs[count : 2 * count], refs[2 * count]
+    sol_ref, new_ref = refs[2 * count + 1 :]
+    total = product(residuals[0][...], alphas[0])
+    for res_ref, alpha_ref in zip(residuals[1:], alphas[1:]):
+        total = total + product(res_ref[...], alpha_ref)
+    sol_ref[...] = total
+    new_ref[...] = residuals[-1][...] - product(image_ref[...], alphas[-1])
+
+
+def last_update(residuals, alphas, image):
+    rows, width = image.shape
+    count = len(residuals)
+    shape = jax.ShapeDtypeStruct(image.shape, jnp.float32)
+    return pl.pallas_call(
+        functools.partial(last_kernel, count),
+        grid=(rows // TILE,),
+        out_shape=(shape, shape),
+        in_specs=[tiles(width)] * count + [WHOLE] * count + [tiles(width)],
+        out_specs=(tiles(width), tiles(width)),
+        name="last_update",
+    )(*residuals, *alphas, image)
+
+
 def shards(rhs, near_blocks, source_basis, target_basis, far_coupling, send_ids, far_list):
     rows, width = rhs.shape
     rank = source_basis.shape[1]
     leaves = rows // LEAF
-    fanout = far_list.shape[1] // leaves
     senders = send_ids[0].reshape(-1)
     readers = far_list[0]
     source_leaf = source_basis.reshape(leaves, LEAF, rank)
-    target_leaf = target_basis.reshape(leaves, LEAF, rank)
-    solution = jnp.zeros_like(rhs)
+    target_t = target_basis.T
+    n_blk = lax.axis_size("blk")
+    n = lax.axis_size("wide") * n_blk
     residual = rhs
+    vb = rhs.astype(jnp.bfloat16)
+    residuals, alphas = [], []
     for step in range(ITERS):
-        vb = residual.astype(jnp.bfloat16)
-        ext = with_halo(vb, (("blk", 0),), HALO)
         coef = jnp.einsum(
             "lia,lis->las",
             source_leaf,
@@ -221,27 +363,15 @@
         incoming = lax.all_to_all(
             outgoing, ("wide", "blk"), split_axis=0, concat_axis=0, tiled=True
         )
-        near = near_apply(near_blocks, ext)
-        picked = incoming[readers].reshape(leaves, fanout, rank, width)
-        trans = jnp.einsum(
-            "lfab,lfbs->las", far_coupling, picked, preferred_element_type=jnp.float32
-        ).astype(jnp.bfloat16)
-        far = jnp.einsum(
-            "lia,las->lis", target_leaf, trans, preferred_element_type=jnp.float32
-        ).reshape(rows, width)
-        image = residual + near + far
-        local_gram = jnp.einsum("rs,rt->st", image, image, precision=lax.Precision.HIGHEST)
-        local_proj = jnp.einsum("rs,rt->st", image, residual, precision=lax.Precision.HIGHEST)
-        half = width // 2
-        part = jnp.concatenate(
-            [local_gram[:, :half], local_gram[:, half:], local_proj[:, :half], local_proj[:, half:]], axis=0
-        )
-        n_blk = lax.axis_size("blk")
-        both = sum_over_devices(part, lax.axis_size("wide") * n_blk, n_blk)
-        alpha = solve(both, width)
-        solution = solution + jnp.dot(residual, alpha, precision=lax.Precision.HIGHEST)
-        residual = residual - jnp.dot(image, alpha, precision=lax.Precision.HIGHEST)
-    return (solution, residual)
+        before, after = sides(vb, "blk", HALO)
+        base = near_base(near_blocks, vb, before, after, residual)
+        image, part = image_and_sums(readers, base, residual, incoming, far_coupling, target_t)
+        both = sum_over_devices(part, n, n_blk)
+        residuals.append(residual)
+        alphas.append(solve(both, width))
+        if step < ITERS - 1:
+            residual, vb = update(residual, image, alphas[-1])
+    return last_update(residuals, alphas, image)
 
 
 def solution(mesh):

time: 255 us -> 217 us (0.85)
  matrix products: 94.4 us -> 3.65 us
  Pallas kernels: 95.7 us -> 162 us
  waiting for transfers between devices: 2.38 us -> 22.2 us
  local copies, waits for them, and re-layouts: 27.9 us -> 8.38 us
  other arithmetic: 14.3 us -> 3.11 us
    dot_general x18 -> x0, matrix products: 91.6 us -> none  [the longest x8 27.9 us: near_apply(): jnp.dot(near_rows[j * NEAR:(j + 1) * NEAR], ext[j * NEAR:j * NEAR + NEAR...]
    pallas_call x0 -> x6, Pallas kernels: none -> 71.3 us  [the longest x2 25.5 us: image_and_sums(): pl.pallas_call(functools.partial(image_kernel, fanout), grid=(rows // TIL...]
    ppermute x4, waiting for transfers between devices: 0.97 us -> 22.2 us  [the longest x2 22.2 us: sides(): lax.ppermute(value[:width], axis, down)]
    unnamed x40 -> x14, local copies, waits for them, and re-layouts: 12.7 us -> 2.97 us
    add x2 -> x0, other arithmetic: 9.5 us -> none  [shards(): image = residual + near + far]
    reshape x1 -> x0, local copies, waits for them, and re-layouts: 5.74 us -> none  [shards(): far = jnp.einsum('lia,las->lis', target_leaf, trans, preferred_element_ty...]
    pallas_call x2, Pallas kernels: 70.5 us -> 65.8 us  [sum_over_devices(): pl.pallas_call(functools.partial(sum_kernel, n, n_blk), out_shape=jax.Sha...]
    gather x2 -> x0, local copies, waits for them, and re-layouts: 3.67 us -> none  [shards(): picked = incoming[readers].reshape(leaves, fanout, rank, width)]
  transfers between devices with their start and end apart: 6 -> 6, of which waited for: 3 -> 2; matrix products, arithmetic and copies ran while one was open for 17% -> 0% of each run, Pallas kernels for 0% -> 11%
where the time goes in v2:
time: 217 us; the launch traced here: 215 us
  Pallas kernels  162 us (75%)
  waiting for transfers between devices  22.2 us (10%)
  starting transfers between devices  15.3 us (7%)
  local copies, waits for them, and re-layouts  8.38 us (4%)
  matrix products  3.65 us (2%)
  other arithmetic  3.11 us (1%)
    pallas_call x2, Pallas kernels, sum_over_devices(): pl.pallas_call(functools.partial(sum_kernel, n, n_blk), out_shape=jax.Sha...  65.8 us
    pallas_call x2, Pallas kernels, image_and_sums(): pl.pallas_call(functools.partial(image_kernel, fanout), grid=(rows // TIL...  25.5 us
    pallas_call x2, Pallas kernels, solve(): pl.pallas_call(solve_kernel, out_shape=jax.ShapeDtypeStruct((width, width...  24.8 us
    pallas_call x2, Pallas kernels, near_base(): pl.pallas_call(near_kernel, grid=(rows // TILE,), out_shape=jax.ShapeDtyp...  24.1 us
    ppermute x2, waiting for transfers between devices, sides(): lax.ppermute(value[:width], axis, down)  22.2 us
    pallas_call x1, Pallas kernels, last_update(): pl.pallas_call(functools.partial(last_kernel, count), grid=(rows // TILE,...  12.2 us
    all_to_all x2, starting transfers between devices, shards(): lax.all_to_all(outgoing, ('wide', 'blk'), split_axis=0, concat_axis=0, ti...  11.7 us
    pallas_call x1, Pallas kernels, update(): pl.pallas_call(update_kernel, grid=(rows // TILE,), out_shape=(jax.ShapeD...  9.43 us
  transfers between devices with their start and end apart: 6, of which 2 were waited for; matrix products, arithmetic and copies ran while one was open for 0% of the time, Pallas kernels for 11%

profile of v2, /device:TPU:29, one launch (start us, length us, event | category | flops | bytes accessed | tf_op | source)
XLA Modules:
  0.0 215.2 jit_solution(18383649163598871628)
XLA Ops:
  0.6 0.0 copy-start
  0.6 0.7 fusion.5
  1.4 2.4 %convert_element_type.12.vb_ref = bf16[4096,256]{1,0:T(8,128)(2,1)S(1)} convert(f32[4096,256]{1,0:T(8,128)} %refs_0_.1) | non-fusion elementwise | flops 1048576 | bytes 6291456 | tf_op jit(solution)/shard_map/convert_element_type | solution.py:353
  3.8 0.0 copy-start.1
  3.8 0.0 copy-done
  3.8 1.6 convolution_convert_fusion.1
  5.4 2.8 %gather_fusion = bf16[32,64,256]{2,1,0:T(8,128)(2,1)} fusion(bf16[32,64,256]{2,1,0:T(8,128)(2,1)} %convolution_convert_fusion.1, s32[1024]{0:T(1024)S(1)} %pad_clamp_fusion), kind=kCustom, calls=%fused_computation | custom fusion | bytes 2097280 | tf_op jit(solution)/shard_map/gather | solution.py:362
  8.2 6.2 %all-to-all-start = ((bf16[32,64,256]{2,1,0:T(8,128)(2,1)}), bf16[32,64,256]{2,1,0:T(8,128)(2,1)}, u32[]{:S(2)}, u32[]{:S(2)}) async-start(bf16[32,64,256]{2,1,0:T(8,128)(2,1)} %gather_fusion), calls=%async_computation | async-start | bytes 2097152 | tf_op jit(solution)/shard_map/all_to_all | solution.py:363
  14.4 0.0 copy-done.1
  14.5 0.4 collective-permute-start.1
  14.9 1.4 collective-permute-start
  16.3 11.5 %collective-permute-done.1.after_ref = bf16[256,256]{1,0:T(8,128)(2,1)S(1)} collective-permute-done((bf16[256,256]{1,0:T(8,128)(2,1)S(1)}, bf16[256,256]{1,0:T(8,128)(2,1)S(1)}, u32[]{:S(2)}, u32[]{:S(2)}) %collective-permute-start.1) | collective-permute-done | bytes 131104 | tf_op jit(solution)/shard_map/ppermute | solution.py:20
  27.8 0.0 copy-start.4
  27.8 0.0 collective-permute-done.before_ref
  27.8 0.6 copy-done.4
  28.4 0.0 copy-start.6
  28.4 0.6 copy-done.6
  29.1 12.1 %near.2.base_ref = f32[4096,256]{1,0:T(8,128)} custom-call(bf16[4096,1536]{1,0:T(8,128)(2,1)} %near_ref.3, bf16[4096,256]{1,0:T(8,128)(2,1)} %copy-done.1, bf16[256,256]{1,0:T(8,128)(2,1)} %copy-done.6, bf16[256,256]{1,0:T(8,128)(2,1)} %copy-done.4, f32[4096,256]{1,0:T(8,128)} %refs_0_.1), custom_call_target="tpu_custom_call" | custom-call | flops 3221225472 | bytes 20971520 | tf_op jit(solution)/shard_map/near/pallas_call | solution.py:218
  41.1 0.0 all-to-all-done.incoming_ref
  41.1 12.8 %image.2 = (f32[4096,256]{1,0:T(8,128)}, f32[1024,128]{1,0:T(8,128)}) custom-call(s32[32]{0:T(128)} %bitcast.28, f32[4096,256]{1,0:T(8,128)} %near.2.base_ref, f32[4096,256]{1,0:T(8,128)} %refs_0_.1, bf16[32,64,256]{2,1,0:T(8,128)(2,1)} %all-to-all-done.incoming_ref, bf16[32,1,64,64]{3,2,1,0:T(8,128)(2,1)} %coupling_ref.3, bf16[64,4096]{1,0:T(8,128)(2,1)} %bitcast.26), custom_call_target="tpu_custom_call" | custom-call | tf_op jit(solution)/shard_map/image/pallas_call | solution.py:270
  53.9 32.8 %sum_over_devices.2.both_ref = f32[1024,128]{1,0:T(8,128)} custom-call(f32[1024,128]{1,0:T(8,128)} %get-tuple-element.9.part_ref), custom_call_target="tpu_custom_call" | custom-call | tf_op jit(solution)/shard_map/sum_over_devices/pallas_call | solution.py:112
  86.7 12.4 %solve.2.alpha_ref.refs_2_ = f32[256,256]{1,0:T(8,128)} custom-call(f32[1024,128]{1,0:T(8,128)} %sum_over_devices.2.both_ref), custom_call_target="tpu_custom_call" | custom-call | tf_op jit(solution)/shard_map/solve/pallas_call | solution.py:172
  99.1 9.4 %update.1 = (f32[4096,256]{1,0:T(8,128)}, bf16[4096,256]{1,0:T(8,128)(2,1)}) custom-call(f32[4096,256]{1,0:T(8,128)} %refs_0_.1, f32[4096,256]{1,0:T(8,128)} %get-tuple-element.8.image_ref, f32[256,256]{1,0:T(8,128)} %solve.2.alpha_ref.refs_2_), custom_call_target="tpu_custom_call" | custom-call | tf_op jit(solution)/shard_map/update/pallas_call | solution.py:305
  108.5 2.0 fusion
  110.5 1.6 gather_fusion.1
  112.1 5.6 %all-to-all-start.1 = ((bf16[32,64,256]{2,1,0:T(8,128)(2,1)}), bf16[32,64,256]{2,1,0:T(8,128)(2,1)S(1)}, u32[]{:S(2)}, u32[]{:S(2)}) async-start(bf16[32,64,256]{2,1,0:T(8,128)(2,1)} %gather_fusion.1), calls=%async_computation.1 | async-start | bytes 2097152 | tf_op jit(solution)/shard_map/all_to_all | solution.py:363
  117.7 1.0 fusion.6
  118.7 0.4 collective-permute-start.3
  119.1 1.4 collective-permute-start.2
  120.5 10.6 %collective-permute-done.3.after_ref = bf16[256,256]{1,0:T(8,128)(2,1)S(1)} collective-permute-done((bf16[256,256]{1,0:T(8,128)(2,1)S(1)}, bf16[256,256]{1,0:T(8,128)(2,1)S(1)}, u32[]{:S(2)}, u32[]{:S(2)}) %collective-permute-start.3) | collective-permute-done | bytes 131104 | tf_op jit(solution)/shard_map/ppermute | solution.py:20
  131.1 0.0 copy-start.3
  131.1 0.0 collective-permute-done.2.before_ref
  131.1 0.0 copy-start.5
  131.1 0.6 copy-done.3
  131.8 0.1 copy-done.5
  131.8 12.1 %near.3.base_ref = f32[4096,256]{1,0:T(8,128)} custom-call(bf16[4096,1536]{1,0:T(8,128)(2,1)} %near_ref.3, bf16[4096,256]{1,0:T(8,128)(2,1)} %get-tuple-element.11.vb_ref, bf16[256,256]{1,0:T(8,128)(2,1)} %copy-done.5, bf16[256,256]{1,0:T(8,128)(2,1)} %copy-done.3, f32[4096,256]{1,0:T(8,128)} %get-tuple-element.10.res_ref.refs_1_), custom_call_target="tpu_custom_call" | custom-call | flops 3221225472 | bytes 20971520 | tf_op jit(solution)/shard_map/near/pallas_call | solution.py:218
  143.9 0.0 all-to-all-done.1.incoming_ref
  143.9 0.0 copy-start.2
  143.9 1.0 copy-done.2
  144.9 12.8 %image.3 = (f32[4096,256]{1,0:T(8,128)}, f32[1024,128]{1,0:T(8,128)}) custom-call(s32[32]{0:T(128)} %bitcast.29, f32[4096,256]{1,0:T(8,128)} %near.3.base_ref, f32[4096,256]{1,0:T(8,128)} %get-tuple-element.10.res_ref.refs_1_, bf16[32,64,256]{2,1,0:T(8,128)(2,1)} %copy-done.2, bf16[32,1,64,64]{3,2,1,0:T(8,128)(2,1)} %coupling_ref.3, bf16[64,4096]{1,0:T(8,128)(2,1)} %bitcast.27), custom_call_target="tpu_custom_call" | custom-call | tf_op jit(solution)/shard_map/image/pallas_call | solution.py:270
  157.6 33.0 %sum_over_devices.3.both_ref = f32[1024,128]{1,0:T(8,128)} custom-call(f32[1024,128]{1,0:T(8,128)} %get-tuple-element.12.part_ref), custom_call_target="tpu_custom_call" | custom-call | tf_op jit(solution)/shard_map/sum_over_devices/pallas_call | solution.py:112
  190.6 12.4 %solve.3.refs_3_ = f32[256,256]{1,0:T(8,128)} custom-call(f32[1024,128]{1,0:T(8,128)} %sum_over_devices.3.both_ref), custom_call_target="tpu_custom_call" | custom-call | tf_op jit(solution)/shard_map/solve/pallas_call | solution.py:172
  203.0 12.2 %last_update.1 = (f32[4096,256]{1,0:T(8,128)}, f32[4096,256]{1,0:T(8,128)}) custom-call(f32[4096,256]{1,0:T(8,128)} %refs_0_.1, f32[4096,256]{1,0:T(8,128)} %get-tuple-element.10.res_ref.refs_1_, f32[256,256]{1,0:T(8,128)} %solve.2.alpha_ref.refs_2_, f32[256,256]{1,0:T(8,128)} %solve.3.refs_3_, f32[4096,256]{1,0:T(8,128)} %get-tuple-element.13.refs_4_), custom_call_target="tpu_custom_call" | custom-call | tf_op jit(solution)/shard_map/last_update/pallas_call | solution.py:332
  (2 shorter events, 0.0 us)
Async XLA Ops:
  0.6 3.1 %copy-start = (bf16[4096,64]{0,1:T(8,128)(2,1)S(1)}, bf16[4096,64]{0,1:T(8,128)(2,1)}, u32[]{:S(2)}) copy-start(bf16[4096,64]{0,1:T(8,128)(2,1)} %param.9) | copy-start | bytes 1572868
  3.8 10.7 %copy-start.1 = (bf16[4096,256]{1,0:T(8,128)(2,1)}, bf16[4096,256]{1,0:T(8,128)(2,1)S(1)}, u32[]{:S(2)}) copy-start(bf16[4096,256]{1,0:T(8,128)(2,1)S(1)} %convert_element_type.12.vb_ref) | copy-start | bytes 6291460
  8.2 32.9 %all-to-all-start = ((bf16[32,64,256]{2,1,0:T(8,128)(2,1)}), bf16[32,64,256]{2,1,0:T(8,128)(2,1)}, u32[]{:S(2)}, u32[]{:S(2)}) async-start(bf16[32,64,256]{2,1,0:T(8,128)(2,1)} %gather_fusion), calls=%async_computation | async-start | bytes 2097152 | tf_op jit(solution)/shard_map/all_to_all | solution.py:363
  14.5 13.3 %collective-permute-start.1 = (bf16[256,256]{1,0:T(8,128)(2,1)S(1)}, bf16[256,256]{1,0:T(8,128)(2,1)S(1)}, u32[]{:S(2)}, u32[]{:S(2)}) collective-permute-start(bf16[256,256]{1,0:T(8,128)(2,1)S(1)} %get-tuple-element.16), channel_id=1, source_target_pairs={{1,0},{2,1},{3,2},{4,3},{5,4},{6,5},{7,6},{0,7},{9,8},{10,9},{11,1... | collective-permute-start | bytes 393224 | tf_op jit(solution)/shard_map/ppermute | solution.py:20
  14.9 12.9 %collective-permute-start = (bf16[256,256]{1,0:T(8,128)(2,1)S(1)}, bf16[256,256]{1,0:T(8,128)(2,1)S(1)}, u32[]{:S(2)}, u32[]{:S(2)}) collective-permute-start(bf16[256,256]{1,0:T(8,128)(2,1)S(1)} %get-tuple-element.17), channel_id=1, source_target_pairs={{0,1},{1,2},{2,3},{3,4},{4,5},{5,6},{6,7},{7,0},{8,9},{9,10},{10,1... | collective-permute-start | bytes 393224 | tf_op jit(solution)/shard_map/ppermute | solution.py:20
  27.8 0.6 copy-start.4
  28.4 0.6 copy-start.6
  112.1 31.8 %all-to-all-start.1 = ((bf16[32,64,256]{2,1,0:T(8,128)(2,1)}), bf16[32,64,256]{2,1,0:T(8,128)(2,1)S(1)}, u32[]{:S(2)}, u32[]{:S(2)}) async-start(bf16[32,64,256]{2,1,0:T(8,128)(2,1)} %gather_fusion.1), calls=%async_computation.1 | async-start | bytes 2097152 | tf_op jit(solution)/shard_map/all_to_all | solution.py:363
  118.7 12.4 %collective-permute-start.3 = (bf16[256,256]{1,0:T(8,128)(2,1)S(1)}, bf16[256,256]{1,0:T(8,128)(2,1)S(1)}, u32[]{:S(2)}, u32[]{:S(2)}) collective-permute-start(bf16[256,256]{1,0:T(8,128)(2,1)S(1)} %get-tuple-element.14), channel_id=1, source_target_pairs={{1,0},{2,1},{3,2},{4,3},{5,4},{6,5},{7,6},{0,7},{9,8},{10,9},{11,1... | collective-permute-start | bytes 393224 | tf_op jit(solution)/shard_map/ppermute | solution.py:20
  119.1 12.0 %collective-permute-start.2 = (bf16[256,256]{1,0:T(8,128)(2,1)S(1)}, bf16[256,256]{1,0:T(8,128)(2,1)S(1)}, u32[]{:S(2)}, u32[]{:S(2)}) collective-permute-start(bf16[256,256]{1,0:T(8,128)(2,1)S(1)} %get-tuple-element.15), channel_id=1, source_target_pairs={{0,1},{1,2},{2,3},{3,4},{4,5},{5,6},{6,7},{7,0},{8,9},{9,10},{10,1... | collective-permute-start | bytes 393224 | tf_op jit(solution)/shard_map/ppermute | solution.py:20
  131.1 0.6 copy-start.3
  131.1 0.7 copy-start.5
  143.9 1.0 copy-start.2

commit v3 on v2

--- a/solution.py
+++ b/solution.py
@@ -24,104 +24,120 @@
     return jnp.dot(a, b, precision=lax.Precision.HIGHEST, preferred_element_type=jnp.float32)
 
 
-def sum_kernel(n, n_blk, part_ref, out_ref, landed, total, sent, got, sent2, got2):
+def sum_kernel(n, n_blk, part_ref, out_ref, other, mine, landed, total, pair_sem, sent, got, sent2, got2, sent3, got3):
     me = lax.axis_index("wide") * n_blk + lax.axis_index("blk")
-    chunk = part_ref.shape[0] // n
+    m = n // 2
+    half = part_ref.shape[0] // 2
+    chunk = half // m
+    side = lax.rem(me, 2)
+    idx = me // 2
+    partner = me + 1 - 2 * side
 
     def peer_of(d):
-        return lax.rem(me + d, n)
+        return lax.rem(idx + d, m)
 
     def place(p):
         return {"wide": p // n_blk, "blk": lax.rem(p, n_blk)}
 
-    def rows(p):
-        return pl.ds(pl.multiple_of(p * chunk, chunk), chunk)
-
-    barrier = pltpu.get_barrier_semaphore()
-
-    def greet(d, c):
-        pl.semaphore_signal(barrier, inc=1, device_id=place(peer_of(d)), device_id_type=pl.DeviceIdType.MESH)
-        return c
-
-    lax.fori_loop(1, n, greet, 0)
-    pl.semaphore_wait(barrier, n - 1)
-
-    def scatter(d):
-        p = peer_of(d)
+    def rows(start, size):
+        return pl.ds(pl.multiple_of(start, size), size)
+
+    def send(src, dst, send_sem, recv_sem, device):
         return pltpu.make_async_remote_copy(
-            src_ref=part_ref.at[rows(p)],
-            dst_ref=landed.at[rows(me)],
-            send_sem=sent.at[d],
-            recv_sem=got.at[me],
-            device_id=place(p),
+            src_ref=src,
+            dst_ref=dst,
+            send_sem=send_sem,
+            recv_sem=recv_sem,
+            device_id=place(device),
             device_id_type=pl.DeviceIdType.MESH,
         )
 
+    barrier = pltpu.get_barrier_semaphore()
+
+    def greet(d, c):
+        pl.semaphore_signal(
+            barrier, inc=1, device_id=place(2 * peer_of(d) + side), device_id_type=pl.DeviceIdType.MESH
+        )
+        return c
+
+    pl.semaphore_signal(barrier, inc=1, device_id=place(partner), device_id_type=pl.DeviceIdType.MESH)
+    lax.fori_loop(1, m, greet, 0)
+    pl.semaphore_wait(barrier, m)
+
+    pair = send(part_ref.at[rows((1 - side) * half, half)], other, pair_sem.at[0], pair_sem.at[1], partner)
+    pair.start()
+    pair.wait()
+    mine[...] = part_ref[rows(side * half, half)] + other[...]
+
+    def scatter(d):
+        q = peer_of(d)
+        return send(mine.at[rows(q * chunk, chunk)], landed.at[rows(idx * chunk, chunk)], sent.at[d], got.at[idx], 2 * q + side)
+
+    def own(q):
+        return total.at[rows(side * half + q * chunk, chunk)]
+
     def gather(d):
-        p = peer_of(d)
-        return pltpu.make_async_remote_copy(
-            src_ref=total.at[rows(me)],
-            dst_ref=total.at[rows(me)],
-            send_sem=sent2.at[d],
-            recv_sem=got2.at[me],
-            device_id=place(p),
-            device_id_type=pl.DeviceIdType.MESH,
-        )
-
-    def arrived(ref, sems, d):
-        p = peer_of(d)
-        return pltpu.make_async_remote_copy(
-            src_ref=ref.at[rows(p)],
-            dst_ref=ref.at[rows(p)],
-            send_sem=sent.at[d],
-            recv_sem=sems.at[p],
-            device_id=place(p),
-            device_id_type=pl.DeviceIdType.MESH,
-        )
+        return send(own(idx), own(idx), sent2.at[d], got2.at[idx], 2 * peer_of(d) + side)
+
+    def forward(q):
+        return send(own(q), own(q), sent3.at[q], got3.at[q], partner)
 
     def start1(d, c):
         scatter(d).start()
         return c
 
-    lax.fori_loop(1, n, start1, 0)
+    lax.fori_loop(1, m, start1, 0)
 
     def add(d, acc):
-        arrived(landed, got, d).wait_recv()
-        return acc + landed[rows(peer_of(d))]
-
-    acc = lax.fori_loop(1, n, add, part_ref[rows(me)])
-    total[rows(me)] = acc
+        q = peer_of(d)
+        slot = landed.at[rows(q * chunk, chunk)]
+        send(slot, slot, sent.at[d], got.at[q], 2 * q + side).wait_recv()
+        return acc + landed[rows(q * chunk, chunk)]
+
+    total[rows(side * half + idx * chunk, chunk)] = lax.fori_loop(1, m, add, mine[rows(idx * chunk, chunk)])
 
     def start2(d, c):
         gather(d).start()
         return c
 
-    lax.fori_loop(1, n, start2, 0)
+    lax.fori_loop(1, m, start2, 0)
+    forward(idx).start()
+
+    def relay(d, c):
+        q = peer_of(d)
+        send(own(q), own(q), sent2.at[d], got2.at[q], 2 * q + side).wait_recv()
+        forward(q).start()
+        return c
+
+    lax.fori_loop(1, m, relay, 0)
 
     def drain(d, c):
         scatter(d).wait_send()
         gather(d).wait_send()
-        arrived(total, got2, d).wait_recv()
-        return c
-
-    lax.fori_loop(1, n, drain, 0)
+        return c
+
+    lax.fori_loop(1, m, drain, 0)
+
+    def finish(q, c):
+        forward(q).wait_send()
+        slot = total.at[rows((1 - side) * half + q * chunk, chunk)]
+        send(slot, slot, sent3.at[q], got3.at[q], partner).wait_recv()
+        return c
+
+    lax.fori_loop(0, m, finish, 0)
     out_ref[...] = total[...]
 
 
 def sum_over_devices(part, n, n_blk):
+    half = (part.shape[0] // 2, part.shape[1])
     return pl.pallas_call(
         functools.partial(sum_kernel, n, n_blk),
         out_shape=jax.ShapeDtypeStruct(part.shape, part.dtype),
         in_specs=[pl.BlockSpec(memory_space=pltpu.VMEM)],
         out_specs=pl.BlockSpec(memory_space=pltpu.VMEM),
-        scratch_shapes=[
-            pltpu.VMEM(part.shape, part.dtype),
-            pltpu.VMEM(part.shape, part.dtype),
-            pltpu.SemaphoreType.DMA((n,)),
-            pltpu.SemaphoreType.DMA((n,)),
-            pltpu.SemaphoreType.DMA((n,)),
-            pltpu.SemaphoreType.DMA((n,)),
-        ],
+        scratch_shapes=[pltpu.VMEM(half, part.dtype)] * 3
+        + [pltpu.VMEM(part.shape, part.dtype), pltpu.SemaphoreType.DMA((2,))]
+        + [pltpu.SemaphoreType.DMA((n // 2,))] * 6,
         compiler_params=pltpu.CompilerParams(collective_id=0, has_side_effects=True),
         name="sum_over_devices",
     )(part)
@@ -199,37 +215,37 @@
     return pl.BlockSpec((TILE, width), lambda i: (i, 0))
 
 
-def near_kernel(near_ref, vb_ref, before_ref, after_ref, res_ref, out_ref, ext):
+def near_kernel(near_ref, vb_ref, res_ref, out_ref, ext):
     i = pl.program_id(0)
-    halo, rows = before_ref.shape[0], vb_ref.shape[0]
+    rows, width = vb_ref.shape
 
     @pl.when(i == 0)
     def _():
-        ext[:halo] = before_ref[...]
-        ext[halo : halo + rows] = vb_ref[...]
-        ext[halo + rows :] = after_ref[...]
+        ext[:HALO] = jnp.zeros((HALO, width), ext.dtype)
+        ext[HALO : HALO + rows] = vb_ref[...]
+        ext[HALO + rows :] = jnp.zeros((HALO, width), ext.dtype)
 
     start = pl.multiple_of((i * TILE) // NEAR * NEAR, NEAR)
     out_ref[...] = res_ref[...] + dot16(near_ref[...], ext[pl.ds(start, near_ref.shape[1])])
 
 
-def near_base(near_blocks, vb, before, after, residual):
+def near_base(near_blocks, vb, residual):
     rows, width = residual.shape
     return pl.pallas_call(
         near_kernel,
         grid=(rows // TILE,),
         out_shape=jax.ShapeDtypeStruct(residual.shape, jnp.float32),
-        in_specs=[tiles(near_blocks.shape[1]), WHOLE, WHOLE, WHOLE, tiles(width)],
+        in_specs=[tiles(near_blocks.shape[1]), WHOLE, tiles(width)],
         out_specs=tiles(width),
         scratch_shapes=[pltpu.VMEM((rows + 2 * HALO, width), jnp.bfloat16)],
         cost_estimate=pl.CostEstimate(
             flops=2 * rows * near_blocks.shape[1] * width, bytes_accessed=2 * near_blocks.size + 8 * residual.size, transcendentals=0
         ),
         name="near",
-    )(near_blocks, vb, before, after, residual)
-
-
-def image_kernel(fanout, list_ref, base_ref, res_ref, incoming_ref, coupling_ref, target_ref, image_ref, part_ref, cross):
+    )(near_blocks, vb, residual)
+
+
+def image_kernel(fanout, list_ref, base_ref, res_ref, incoming_ref, coupling_ref, target_ref, first_ref, last_ref, before_ref, after_ref, image_ref, part_ref, cross):
     i = pl.program_id(0)
     width = base_ref.shape[1]
     half = width // 2
@@ -246,6 +262,15 @@
             trans = trans + dot16(coupling_ref[l, f], incoming_ref[list_ref[(i * leaves + l) * fanout + f]])
         far = tdot16(target_ref[:, l * LEAF : (l + 1) * LEAF], trans.astype(jnp.bfloat16))
         image_ref[l * LEAF : (l + 1) * LEAF] = base_ref[l * LEAF : (l + 1) * LEAF] + far
+
+    @pl.when(i < NEAR // TILE)
+    def _():
+        image_ref[...] += dot16(first_ref[...], before_ref[...])
+
+    @pl.when(i >= pl.num_programs(0) - NEAR // TILE)
+    def _():
+        image_ref[...] += dot16(last_ref[...], after_ref[...])
+
     high, low = split(image_ref[...])
     res_high, res_low = split(res_ref[...])
     gram = tdot16(high, high)
@@ -263,10 +288,12 @@
         part_ref[width : 2 * width] += both[:, half:]
 
 
-def image_and_sums(readers, base, residual, incoming, coupling, target_t):
+def image_and_sums(readers, base, residual, incoming, coupling, target_t, near_blocks, before, after):
     rows, width = residual.shape
     leaves, fanout, rank, _ = coupling.shape
     step = TILE // LEAF
+    edge, steps = NEAR // TILE, rows // TILE
+    last_column = near_blocks.shape[1] // HALO - 1
     return pl.pallas_call(
         functools.partial(image_kernel, fanout),
         grid=(rows // TILE,),
@@ -281,11 +308,15 @@
             WHOLE,
             pl.BlockSpec((step, fanout, rank, rank), lambda i: (i, 0, 0, 0)),
             pl.BlockSpec((rank, TILE), lambda i: (0, i)),
+            pl.BlockSpec((TILE, HALO), lambda i: (jnp.minimum(i, edge - 1), 0)),
+            pl.BlockSpec((TILE, HALO), lambda i: (jnp.maximum(i, steps - edge), last_column)),
+            WHOLE,
+            WHOLE,
         ],
         out_specs=(tiles(width), pl.BlockSpec((4 * width, width // 2), lambda i: (0, 0))),
         scratch_shapes=[pltpu.VMEM((width, width), jnp.float32)],
         name="image",
-    )(readers, base, residual, incoming, coupling, target_t)
+    )(readers, base, residual, incoming, coupling, target_t, near_blocks, near_blocks, before, after)
 
 
 def product(x, alpha_ref):
@@ -364,8 +395,10 @@
             outgoing, ("wide", "blk"), split_axis=0, concat_axis=0, tiled=True
         )
         before, after = sides(vb, "blk", HALO)
-        base = near_base(near_blocks, vb, before, after, residual)
-        image, part = image_and_sums(readers, base, residual, incoming, far_coupling, target_t)
+        base = near_base(near_blocks, vb, residual)
+        image, part = image_and_sums(
+            readers, base, residual, incoming, far_coupling, target_t, near_blocks, before, after
+        )
         both = sum_over_devices(part, n, n_blk)
         residuals.append(residual)
         alphas.append(solve(both, width))

time: 217 us -> 199 us (0.917)
  Pallas kernels: 162 us -> 148 us
  waiting for transfers between devices: 22.2 us -> 19.3 us
    ppermute x2, waiting for transfers between devices: 22.2 us -> 0.01 us  [sides(): lax.ppermute(value[:width], axis, down)]
    all_to_all x2, waiting for transfers between devices: 0.01 us -> 19.3 us  [shards(): lax.all_to_all(outgoing, ('wide', 'blk'), split_axis=0, concat_axis=0, ti...]
    pallas_call x2, Pallas kernels: 65.8 us -> 50.7 us  [sum_over_devices(): pl.pallas_call(functools.partial(sum_kernel, n, n_blk), out_shape=jax.Sha...]
  transfers between devices with their start and end apart: 6 -> 6, of which waited for: 2 -> 2; matrix products, arithmetic and copies ran while one was open for 0% -> 1% of each run, Pallas kernels for 11% -> 12%
where the time goes in v3:
time: 199 us; the launch traced here: 196 us
  Pallas kernels  148 us (74%)
  waiting for transfers between devices  19.3 us (10%)
  starting transfers between devices  14.7 us (7%)
  local copies, waits for them, and re-layouts  6.41 us (3%)
  matrix products  3.65 us (2%)
  other arithmetic  3.11 us (2%)
    pallas_call x2, Pallas kernels, sum_over_devices(): pl.pallas_call(functools.partial(sum_kernel, n, n_blk), out_shape=jax.Sha...  50.7 us
    pallas_call x2, Pallas kernels, image_and_sums(): pl.pallas_call(functools.partial(image_kernel, fanout), grid=(rows // TIL...  27.3 us
    pallas_call x2, Pallas kernels, solve(): pl.pallas_call(solve_kernel, out_shape=jax.ShapeDtypeStruct((width, width...  24.8 us
    pallas_call x2, Pallas kernels, near_base(): pl.pallas_call(near_kernel, grid=(rows // TILE,), out_shape=jax.ShapeDtyp...  24 us
    all_to_all x2, waiting for transfers between devices, shards(): lax.all_to_all(outgoing, ('wide', 'blk'), split_axis=0, concat_axis=0, ti...  19.3 us
    pallas_call x1, Pallas kernels, last_update(): pl.pallas_call(functools.partial(last_kernel, count), grid=(rows // TILE,...  12.2 us
    all_to_all x2, starting transfers between devices, shards(): lax.all_to_all(outgoing, ('wide', 'blk'), split_axis=0, concat_axis=0, ti...  11.1 us
    pallas_call x1, Pallas kernels, update(): pl.pallas_call(update_kernel, grid=(rows // TILE,), out_shape=(jax.ShapeD...  9.43 us
  transfers between devices with their start and end apart: 6, of which 2 were waited for; matrix products, arithmetic and copies ran while one was open for 1% of the time, Pallas kernels for 12%

profile of v3, /device:TPU:29, one launch (start us, length us, event | category | flops | bytes accessed | tf_op | source)
XLA Modules:
  0.0 196.3 jit_solution(12357756118454253034)
XLA Ops:
  0.6 0.0 copy-start
  0.6 0.7 fusion.5
  1.4 2.4 %convert_element_type.12.vb_ref = bf16[4096,256]{1,0:T(8,128)(2,1)S(1)} convert(f32[4096,256]{1,0:T(8,128)} %refs_0_.1) | non-fusion elementwise | flops 1048576 | bytes 6291456 | tf_op jit(solution)/shard_map/convert_element_type | solution.py:384
  3.8 0.0 copy-start.1
  3.8 0.0 copy-done
  3.8 1.6 convolution_convert_fusion.1
  5.4 2.8 %gather_fusion = bf16[32,64,256]{2,1,0:T(8,128)(2,1)} fusion(bf16[32,64,256]{2,1,0:T(8,128)(2,1)} %convolution_convert_fusion.1, s32[1024]{0:T(1024)S(1)} %pad_clamp_fusion), kind=kCustom, calls=%fused_computation | custom fusion | bytes 2097280 | tf_op jit(solution)/shard_map/gather | solution.py:393
  8.2 6.2 %all-to-all-start = ((bf16[32,64,256]{2,1,0:T(8,128)(2,1)}), bf16[32,64,256]{2,1,0:T(8,128)(2,1)}, u32[]{:S(2)}, u32[]{:S(2)}) async-start(bf16[32,64,256]{2,1,0:T(8,128)(2,1)} %gather_fusion), calls=%async_computation | async-start | bytes 2097152 | tf_op jit(solution)/shard_map/all_to_all | solution.py:394
  14.4 0.0 copy-done.1
  14.5 0.4 collective-permute-start.1
  14.9 1.4 collective-permute-start
  16.3 12.0 %near.2.base_ref = f32[4096,256]{1,0:T(8,128)} custom-call(bf16[4096,1536]{1,0:T(8,128)(2,1)} %last_ref.3, bf16[4096,256]{1,0:T(8,128)(2,1)} %copy-done.1, f32[4096,256]{1,0:T(8,128)} %refs_0_.1), custom_call_target="tpu_custom_call" | custom-call | flops 3221225472 | bytes 20971520 | tf_op jit(solution)/shard_map/near/pallas_call | solution.py:234
  28.3 0.0 collective-permute-done.1.after_ref
  28.3 0.0 copy-start.4
  28.3 0.0 collective-permute-done.before_ref
  28.3 0.0 copy-start.6
  28.3 10.1 %all-to-all-done.incoming_ref = bf16[32,64,256]{2,1,0:T(8,128)(2,1)} async-done(((bf16[32,64,256]{2,1,0:T(8,128)(2,1)}), bf16[32,64,256]{2,1,0:T(8,128)(2,1)}, u32[]{:S(2)}, u32[]{:S(2)}) %all-to-all-start) | async-done | bytes 1048608 | tf_op jit(solution)/shard_map/all_to_all | solution.py:394
  38.4 0.0 copy-done.4
  38.4 0.0 copy-done.6
  38.4 13.7 %image.2 = (f32[4096,256]{1,0:T(8,128)}, f32[1024,128]{1,0:T(8,128)}) custom-call(s32[32]{0:T(128)} %bitcast.28, f32[4096,256]{1,0:T(8,128)} %near.2.base_ref, f32[4096,256]{1,0:T(8,128)} %refs_0_.1, bf16[32,64,256]{2,1,0:T(8,128)(2,1)} %all-to-all-done.incoming_ref, bf16[32,1,64,64]{3,2,1,0:T(8,128)(2,1)} %coupling_ref.3, bf16[64,4096]{1,0:T(8,128)(2,1)} %bitcast.26, ...), custom_call_target="tpu_custom_call" | custom-call | tf_op jit(solution)/shard_map/image/pallas_call | solution.py:297
  52.1 25.3 %sum_over_devices.2.both_ref = f32[1024,128]{1,0:T(8,128)} custom-call(f32[1024,128]{1,0:T(8,128)} %get-tuple-element.9.part_ref), custom_call_target="tpu_custom_call" | custom-call | tf_op jit(solution)/shard_map/sum_over_devices/pallas_call | solution.py:133
  77.4 12.4 %solve.2.alpha_ref.refs_2_ = f32[256,256]{1,0:T(8,128)} custom-call(f32[1024,128]{1,0:T(8,128)} %sum_over_devices.2.both_ref), custom_call_target="tpu_custom_call" | custom-call | tf_op jit(solution)/shard_map/solve/pallas_call | solution.py:188
  89.8 9.4 %update.1 = (f32[4096,256]{1,0:T(8,128)}, bf16[4096,256]{1,0:T(8,128)(2,1)}) custom-call(f32[4096,256]{1,0:T(8,128)} %refs_0_.1, f32[4096,256]{1,0:T(8,128)} %get-tuple-element.8.image_ref, f32[256,256]{1,0:T(8,128)} %solve.2.alpha_ref.refs_2_), custom_call_target="tpu_custom_call" | custom-call | tf_op jit(solution)/shard_map/update/pallas_call | solution.py:336
  99.2 2.0 %fusion = bf16[32,64,256]{2,1,0:T(8,128)(2,1)S(1)} fusion(bf16[32,128,256]{2,1,0:T(8,128)(2,1)} %bitcast.25, bf16[4096,64]{0,1:T(8,128)(2,1)S(1)} %copy-done), kind=kOutput, calls=%fused_computation.4 | convolution fusion | flops 134742016 | bytes 3670016 | tf_op jit(solution)/shard_map/lia,lis->las/dot_general | solution.py:387
  101.3 1.6 gather_fusion.1
  102.8 4.9 %all-to-all-start.1 = ((bf16[32,64,256]{2,1,0:T(8,128)(2,1)}), bf16[32,64,256]{2,1,0:T(8,128)(2,1)S(1)}, u32[]{:S(2)}, u32[]{:S(2)}) async-start(bf16[32,64,256]{2,1,0:T(8,128)(2,1)} %gather_fusion.1), calls=%async_computation.1 | async-start | bytes 2097152 | tf_op jit(solution)/shard_map/all_to_all | solution.py:394
  107.7 1.0 fusion.6
  108.7 0.4 collective-permute-start.3
  109.2 1.4 collective-permute-start.2
  110.5 12.0 %near.3.base_ref = f32[4096,256]{1,0:T(8,128)} custom-call(bf16[4096,1536]{1,0:T(8,128)(2,1)} %last_ref.3, bf16[4096,256]{1,0:T(8,128)(2,1)} %get-tuple-element.11.vb_ref, f32[4096,256]{1,0:T(8,128)} %get-tuple-element.10.res_ref.refs_1_), custom_call_target="tpu_custom_call" | custom-call | flops 3221225472 | bytes 20971520 | tf_op jit(solution)/shard_map/near/pallas_call | solution.py:234
  122.5 0.0 collective-permute-done.3.after_ref
  122.5 0.0 copy-start.3
  122.5 0.0 collective-permute-done.2.before_ref
  122.5 0.0 copy-start.5
  122.5 9.1 %all-to-all-done.1.incoming_ref = bf16[32,64,256]{2,1,0:T(8,128)(2,1)S(1)} async-done(((bf16[32,64,256]{2,1,0:T(8,128)(2,1)}), bf16[32,64,256]{2,1,0:T(8,128)(2,1)S(1)}, u32[]{:S(2)}, u32[]{:S(2)}) %all-to-all-start.1) | async-done | bytes 1048608 | tf_op jit(solution)/shard_map/all_to_all | solution.py:394
  131.7 0.0 copy-done.3
  131.7 0.0 copy-done.5
  131.7 0.0 copy-start.2
  131.7 1.0 copy-done.2
  132.6 13.7 %image.3 = (f32[4096,256]{1,0:T(8,128)}, f32[1024,128]{1,0:T(8,128)}) custom-call(s32[32]{0:T(128)} %bitcast.29, f32[4096,256]{1,0:T(8,128)} %near.3.base_ref, f32[4096,256]{1,0:T(8,128)} %get-tuple-element.10.res_ref.refs_1_, bf16[32,64,256]{2,1,0:T(8,128)(2,1)} %copy-done.2, bf16[32,1,64,64]{3,2,1,0:T(8,128)(2,1)} %coupling_ref.3, ...), custom_call_target="tpu_custom_call" | custom-call | tf_op jit(solution)/shard_map/image/pallas_call | solution.py:297
  146.3 25.3 %sum_over_devices.3.both_ref = f32[1024,128]{1,0:T(8,128)} custom-call(f32[1024,128]{1,0:T(8,128)} %get-tuple-element.12.part_ref), custom_call_target="tpu_custom_call" | custom-call | tf_op jit(solution)/shard_map/sum_over_devices/pallas_call | solution.py:133
  171.7 12.4 %solve.3.refs_3_ = f32[256,256]{1,0:T(8,128)} custom-call(f32[1024,128]{1,0:T(8,128)} %sum_over_devices.3.both_ref), custom_call_target="tpu_custom_call" | custom-call | tf_op jit(solution)/shard_map/solve/pallas_call | solution.py:188
  184.0 12.2 %last_update.1 = (f32[4096,256]{1,0:T(8,128)}, f32[4096,256]{1,0:T(8,128)}) custom-call(f32[4096,256]{1,0:T(8,128)} %refs_0_.1, f32[4096,256]{1,0:T(8,128)} %get-tuple-element.10.res_ref.refs_1_, f32[256,256]{1,0:T(8,128)} %solve.2.alpha_ref.refs_2_, f32[256,256]{1,0:T(8,128)} %solve.3.refs_3_, f32[4096,256]{1,0:T(8,128)} %get-tuple-element.13.refs_4_), custom_call_target="tpu_custom_call" | custom-call | tf_op jit(solution)/shard_map/last_update/pallas_call | solution.py:363
  (2 shorter events, 0.0 us)
Async XLA Ops:
  0.6 3.1 %copy-start = (bf16[4096,64]{0,1:T(8,128)(2,1)S(1)}, bf16[4096,64]{0,1:T(8,128)(2,1)}, u32[]{:S(2)}) copy-start(bf16[4096,64]{0,1:T(8,128)(2,1)} %param.9) | copy-start | bytes 1572868
  3.8 10.7 %copy-start.1 = (bf16[4096,256]{1,0:T(8,128)(2,1)}, bf16[4096,256]{1,0:T(8,128)(2,1)S(1)}, u32[]{:S(2)}) copy-start(bf16[4096,256]{1,0:T(8,128)(2,1)S(1)} %convert_element_type.12.vb_ref) | copy-start | bytes 6291460
  8.2 30.2 %all-to-all-start = ((bf16[32,64,256]{2,1,0:T(8,128)(2,1)}), bf16[32,64,256]{2,1,0:T(8,128)(2,1)}, u32[]{:S(2)}, u32[]{:S(2)}) async-start(bf16[32,64,256]{2,1,0:T(8,128)(2,1)} %gather_fusion), calls=%async_computation | async-start | bytes 2097152 | tf_op jit(solution)/shard_map/all_to_all | solution.py:394
  14.5 13.8 %collective-permute-start.1 = (bf16[256,256]{1,0:T(8,128)(2,1)S(1)}, bf16[256,256]{1,0:T(8,128)(2,1)S(1)}, u32[]{:S(2)}, u32[]{:S(2)}) collective-permute-start(bf16[256,256]{1,0:T(8,128)(2,1)S(1)} %get-tuple-element.16), channel_id=1, source_target_pairs={{1,0},{2,1},{3,2},{4,3},{5,4},{6,5},{7,6},{0,7},{9,8},{10,9},{11,1... | collective-permute-start | bytes 393224 | tf_op jit(solution)/shard_map/ppermute | solution.py:20
  14.9 13.4 %collective-permute-start = (bf16[256,256]{1,0:T(8,128)(2,1)S(1)}, bf16[256,256]{1,0:T(8,128)(2,1)S(1)}, u32[]{:S(2)}, u32[]{:S(2)}) collective-permute-start(bf16[256,256]{1,0:T(8,128)(2,1)S(1)} %get-tuple-element.17), channel_id=1, source_target_pairs={{0,1},{1,2},{2,3},{3,4},{4,5},{5,6},{6,7},{7,0},{8,9},{9,10},{10,1... | collective-permute-start | bytes 393224 | tf_op jit(solution)/shard_map/ppermute | solution.py:20
  28.3 10.2 %copy-start.4 = (bf16[256,256]{1,0:T(8,128)(2,1)}, bf16[256,256]{1,0:T(8,128)(2,1)S(1)}, u32[]{:S(2)}) copy-start(bf16[256,256]{1,0:T(8,128)(2,1)S(1)} %collective-permute-done.1.after_ref) | copy-start | bytes 393220
  28.3 10.1 %copy-start.6 = (bf16[256,256]{1,0:T(8,128)(2,1)}, bf16[256,256]{1,0:T(8,128)(2,1)S(1)}, u32[]{:S(2)}) copy-start(bf16[256,256]{1,0:T(8,128)(2,1)S(1)} %collective-permute-done.before_ref) | copy-start | bytes 393220
  102.8 28.8 %all-to-all-start.1 = ((bf16[32,64,256]{2,1,0:T(8,128)(2,1)}), bf16[32,64,256]{2,1,0:T(8,128)(2,1)S(1)}, u32[]{:S(2)}, u32[]{:S(2)}) async-start(bf16[32,64,256]{2,1,0:T(8,128)(2,1)} %gather_fusion.1), calls=%async_computation.1 | async-start | bytes 2097152 | tf_op jit(solution)/shard_map/all_to_all | solution.py:394
  108.7 13.8 %collective-permute-start.3 = (bf16[256,256]{1,0:T(8,128)(2,1)S(1)}, bf16[256,256]{1,0:T(8,128)(2,1)S(1)}, u32[]{:S(2)}, u32[]{:S(2)}) collective-permute-start(bf16[256,256]{1,0:T(8,128)(2,1)S(1)} %get-tuple-element.14), channel_id=1, source_target_pairs={{1,0},{2,1},{3,2},{4,3},{5,4},{6,5},{7,6},{0,7},{9,8},{10,9},{11,1... | collective-permute-start | bytes 393224 | tf_op jit(solution)/shard_map/ppermute | solution.py:20
  109.2 13.4 %collective-permute-start.2 = (bf16[256,256]{1,0:T(8,128)(2,1)S(1)}, bf16[256,256]{1,0:T(8,128)(2,1)S(1)}, u32[]{:S(2)}, u32[]{:S(2)}) collective-permute-start(bf16[256,256]{1,0:T(8,128)(2,1)S(1)} %get-tuple-element.15), channel_id=1, source_target_pairs={{0,1},{1,2},{2,3},{3,4},{4,5},{5,6},{6,7},{7,0},{8,9},{9,10},{10,1... | collective-permute-start | bytes 393224 | tf_op jit(solution)/shard_map/ppermute | solution.py:20
  122.5 9.2 %copy-start.3 = (bf16[256,256]{1,0:T(8,128)(2,1)}, bf16[256,256]{1,0:T(8,128)(2,1)S(1)}, u32[]{:S(2)}) copy-start(bf16[256,256]{1,0:T(8,128)(2,1)S(1)} %collective-permute-done.3.after_ref) | copy-start | bytes 393220
  122.5 9.1 %copy-start.5 = (bf16[256,256]{1,0:T(8,128)(2,1)}, bf16[256,256]{1,0:T(8,128)(2,1)S(1)}, u32[]{:S(2)}) copy-start(bf16[256,256]{1,0:T(8,128)(2,1)S(1)} %collective-permute-done.2.before_ref) | copy-start | bytes 393220
  131.7 1.0 copy-start.2

commit v4 on v3

--- a/solution.py
+++ b/solution.py
@@ -273,9 +273,10 @@
 
     high, low = split(image_ref[...])
     res_high, res_low = split(res_ref[...])
-    gram = tdot16(high, high)
-    proj = tdot16(high, res_high) + tdot16(high, res_low) + tdot16(low, res_high)
-    cross[...] += tdot16(high, low)
+    sums = tdot16(high, jnp.concatenate([high, low, res_high, res_low], axis=1))
+    gram = sums[:, :width]
+    proj = sums[:, 2 * width : 3 * width] + sums[:, 3 * width :] + tdot16(low, res_high)
+    cross[...] += sums[:, width : 2 * width]
     part_ref[:width] += gram[:, :half]
     part_ref[width : 2 * width] += gram[:, half:]
     part_ref[2 * width : 3 * width] += proj[:, :half]
@@ -325,25 +326,31 @@
     return dot16(high, a_high) + dot16(high, a_low) + dot16(low, a_high)
 
 
-def update_kernel(res_ref, image_ref, alpha_ref, new_ref, vb_ref):
+def update_kernel(res_ref, image_ref, alpha_ref, source_ref, new_ref, vb_ref, coef_ref):
     new = res_ref[...] - product(image_ref[...], alpha_ref)
     new_ref[...] = new
-    vb_ref[...] = new.astype(jnp.bfloat16)
-
-
-def update(residual, image, alpha):
+    vb = new.astype(jnp.bfloat16)
+    vb_ref[...] = vb
+    for l in range(TILE // LEAF):
+        leaf = slice(l * LEAF, (l + 1) * LEAF)
+        coef_ref[l] = dot16(source_ref[:, leaf], vb[leaf]).astype(jnp.bfloat16)
+
+
+def update(residual, image, alpha, source_t):
     rows, width = residual.shape
+    rank, step = source_t.shape[0], TILE // LEAF
     return pl.pallas_call(
         update_kernel,
         grid=(rows // TILE,),
         out_shape=(
             jax.ShapeDtypeStruct(residual.shape, jnp.float32),
             jax.ShapeDtypeStruct(residual.shape, jnp.bfloat16),
+            jax.ShapeDtypeStruct((rows // LEAF, rank, width), jnp.bfloat16),
         ),
-        in_specs=[tiles(width), tiles(width), WHOLE],
-        out_specs=(tiles(width), tiles(width)),
+        in_specs=[tiles(width), tiles(width), WHOLE, pl.BlockSpec((rank, TILE), lambda i: (0, i))],
+        out_specs=(tiles(width), tiles(width), pl.BlockSpec((step, rank, width), lambda i: (i, 0, 0))),
         name="update",
-    )(residual, image, alpha)
+    )(residual, image, alpha, source_t)
 
 
 def last_kernel(count, *refs):
@@ -382,14 +389,11 @@
     n = lax.axis_size("wide") * n_blk
     residual = rhs
     vb = rhs.astype(jnp.bfloat16)
+    coef = jnp.einsum(
+        "lia,lis->las", source_leaf, vb.reshape(leaves, LEAF, width), preferred_element_type=jnp.float32
+    ).astype(jnp.bfloat16)
     residuals, alphas = [], []
     for step in range(ITERS):
-        coef = jnp.einsum(
-            "lia,lis->las",
-            source_leaf,
-            vb.reshape(leaves, LEAF, width),
-            preferred_element_type=jnp.float32,
-        ).astype(jnp.bfloat16)
         outgoing = coef[senders]
         incoming = lax.all_to_all(
             outgoing, ("wide", "blk"), split_axis=0, concat_axis=0, tiled=True
@@ -403,7 +407,7 @@
         residuals.append(residual)
         alphas.append(solve(both, width))
         if step < ITERS - 1:
-            residual, vb = update(residual, image, alphas[-1])
+            residual, vb, coef = update(residual, image, alphas[-1], source_basis.T)
     return last_update(residuals, alphas, image)
 
 

time: 199 us -> 197 us (0.990)
  matrix products: 3.65 us -> 0.43 us
    dot_general x2 -> x1, matrix products: 3.65 us -> 0.43 us  [shards(): jnp.einsum('lia,lis->las', source_leaf, vb.reshape(leaves, LEAF, width),...]
where the time goes in v4:
time: 197 us; the launch traced here: 194 us
  Pallas kernels  149 us (76%)
  waiting for transfers between devices  19.2 us (10%)
  starting transfers between devices  14.6 us (7%)
  local copies, waits for them, and re-layouts  7.4 us (4%)
  other arithmetic  3.11 us (2%)
    pallas_call x2, Pallas kernels, sum_over_devices(): pl.pallas_call(functools.partial(sum_kernel, n, n_blk), out_shape=jax.Sha...  50.6 us
    pallas_call x2, Pallas kernels, image_and_sums(): pl.pallas_call(functools.partial(image_kernel, fanout), grid=(rows // TIL...  27.4 us
    pallas_call x2, Pallas kernels, solve(): pl.pallas_call(solve_kernel, out_shape=jax.ShapeDtypeStruct((width, width...  24.8 us
    pallas_call x2, Pallas kernels, near_base(): pl.pallas_call(near_kernel, grid=(rows // TILE,), out_shape=jax.ShapeDtyp...  24 us
    all_to_all x2, waiting for transfers between devices, shards(): lax.all_to_all(outgoing, ('wide', 'blk'), split_axis=0, concat_axis=0, ti...  19.2 us
    pallas_call x1, Pallas kernels, last_update(): pl.pallas_call(functools.partial(last_kernel, count), grid=(rows // TILE,...  12.2 us
    all_to_all x2, starting transfers between devices, shards(): lax.all_to_all(outgoing, ('wide', 'blk'), split_axis=0, concat_axis=0, ti...  11 us
    pallas_call x1, Pallas kernels, update(): pl.pallas_call(update_kernel, grid=(rows // TILE,), out_shape=(jax.ShapeD...  9.79 us
  transfers between devices with their start and end apart: 6, of which 2 were waited for; matrix products, arithmetic and copies ran while one was open for 1% of the time, Pallas kernels for 12%

profile of v4, /device:TPU:29, one launch (start us, length us, event | category | flops | bytes accessed | tf_op | source)
XLA Modules:
  0.0 194.4 jit_solution(1568884983776791603)
XLA Ops:
  0.6 0.0 copy-start.3
  0.6 0.7 fusion.2
  1.4 2.4 %convert_element_type.6.vb_ref = bf16[4096,256]{1,0:T(8,128)(2,1)S(1)} convert(f32[4096,256]{1,0:T(8,128)} %refs_0_.1) | non-fusion elementwise | flops 1048576 | bytes 6291456 | tf_op jit(solution)/shard_map/convert_element_type | solution.py:391
  3.8 0.0 copy-start
  3.8 0.0 copy-done.3
  3.8 0.4 convolution_convert_fusion
  4.2 1.6 gather_fusion
  5.8 6.1 %all-to-all-start = ((bf16[32,64,256]{2,1,0:T(8,128)(2,1)}), bf16[32,64,256]{2,1,0:T(8,128)(2,1)S(1)}, u32[]{:S(2)}, u32[]{:S(2)}) async-start(bf16[32,64,256]{2,1,0:T(8,128)(2,1)} %gather_fusion), calls=%async_computation | async-start | bytes 2097152 | tf_op jit(solution)/shard_map/all_to_all | solution.py:398
  12.0 0.0 copy-done
  12.0 0.4 collective-permute-start.1
  12.4 1.4 collective-permute-start
  13.8 12.0 %near.2.base_ref = f32[4096,256]{1,0:T(8,128)} custom-call(bf16[4096,1536]{1,0:T(8,128)(2,1)} %last_ref.3, bf16[4096,256]{1,0:T(8,128)(2,1)} %copy-done, f32[4096,256]{1,0:T(8,128)} %refs_0_.1), custom_call_target="tpu_custom_call" | custom-call | flops 3221225472 | bytes 20971520 | tf_op jit(solution)/shard_map/near/pallas_call | solution.py:234
  25.8 0.0 collective-permute-done.1.after_ref
  25.8 0.0 copy-start.5
  25.8 0.0 collective-permute-done.before_ref
  25.8 0.0 copy-start.7
  25.8 10.1 %all-to-all-done.incoming_ref = bf16[32,64,256]{2,1,0:T(8,128)(2,1)S(1)} async-done(((bf16[32,64,256]{2,1,0:T(8,128)(2,1)}), bf16[32,64,256]{2,1,0:T(8,128)(2,1)S(1)}, u32[]{:S(2)}, u32[]{:S(2)}) %all-to-all-start) | async-done | bytes 1048608 | tf_op jit(solution)/shard_map/all_to_all | solution.py:398
  35.9 0.0 copy-start.2
  35.9 0.0 copy-done.5
  35.9 0.0 copy-done.7
  35.9 1.0 copy-done.2
  36.9 13.7 %image.2 = (f32[4096,256]{1,0:T(8,128)}, f32[1024,128]{1,0:T(8,128)}) custom-call(s32[32]{0:T(128)} %bitcast.20, f32[4096,256]{1,0:T(8,128)} %near.2.base_ref, f32[4096,256]{1,0:T(8,128)} %refs_0_.1, bf16[32,64,256]{2,1,0:T(8,128)(2,1)} %copy-done.2, bf16[32,1,64,64]{3,2,1,0:T(8,128)(2,1)} %coupling_ref.3, bf16[64,4096]{1,0:T(8,128)(2,1)} %bitcast.17, ...), custom_call_target="tpu_custom_call" | custom-call | tf_op jit(solution)/shard_map/image/pallas_call | solution.py:298
  50.6 25.3 %sum_over_devices.2.both_ref = f32[1024,128]{1,0:T(8,128)} custom-call(f32[1024,128]{1,0:T(8,128)} %get-tuple-element.10.part_ref), custom_call_target="tpu_custom_call" | custom-call | tf_op jit(solution)/shard_map/sum_over_devices/pallas_call | solution.py:133
  75.9 12.4 %solve.2.alpha_ref.refs_2_ = f32[256,256]{1,0:T(8,128)} custom-call(f32[1024,128]{1,0:T(8,128)} %sum_over_devices.2.both_ref), custom_call_target="tpu_custom_call" | custom-call | tf_op jit(solution)/shard_map/solve/pallas_call | solution.py:188
  88.3 9.8 %update.1 = (f32[4096,256]{1,0:T(8,128)}, bf16[4096,256]{1,0:T(8,128)(2,1)}, bf16[32,64,256]{2,1,0:T(8,128)(2,1)}) custom-call(f32[4096,256]{1,0:T(8,128)} %refs_0_.1, f32[4096,256]{1,0:T(8,128)} %get-tuple-element.9.image_ref, f32[256,256]{1,0:T(8,128)} %solve.2.alpha_ref.refs_2_, bf16[64,4096]{1,0:T(8,128)(2,1)} %bitcast.19), custom_call_target="tpu_custom_call" | custom-call | tf_op jit(solution)/shard_map/update/pallas_call | solution.py:342
  98.1 2.8 %gather_fusion.1 = bf16[32,64,256]{2,1,0:T(8,128)(2,1)} fusion(bf16[32,64,256]{2,1,0:T(8,128)(2,1)} %get-tuple-element.13, s32[1024]{0:T(1024)S(1)} %pad_clamp_fusion), kind=kCustom, calls=%fused_computation.1 | custom fusion | bytes 2097280 | tf_op jit(solution)/shard_map/gather | solution.py:397
  100.9 4.9 %all-to-all-start.1 = ((bf16[32,64,256]{2,1,0:T(8,128)(2,1)}), bf16[32,64,256]{2,1,0:T(8,128)(2,1)S(1)}, u32[]{:S(2)}, u32[]{:S(2)}) async-start(bf16[32,64,256]{2,1,0:T(8,128)(2,1)} %gather_fusion.1), calls=%async_computation.1 | async-start | bytes 2097152 | tf_op jit(solution)/shard_map/all_to_all | solution.py:398
  105.8 1.0 fusion.3
  106.8 0.4 collective-permute-start.3
  107.2 1.4 collective-permute-start.2
  108.6 12.0 %near.3.base_ref = f32[4096,256]{1,0:T(8,128)} custom-call(bf16[4096,1536]{1,0:T(8,128)(2,1)} %last_ref.3, bf16[4096,256]{1,0:T(8,128)(2,1)} %get-tuple-element.12.vb_ref, f32[4096,256]{1,0:T(8,128)} %get-tuple-element.11.res_ref.refs_1_), custom_call_target="tpu_custom_call" | custom-call | flops 3221225472 | bytes 20971520 | tf_op jit(solution)/shard_map/near/pallas_call | solution.py:234
  120.6 0.0 collective-permute-done.3.after_ref
  120.6 0.0 copy-start.4
  120.6 0.0 collective-permute-done.2.before_ref
  120.6 0.0 copy-start.6
  120.6 9.1 %all-to-all-done.1.incoming_ref = bf16[32,64,256]{2,1,0:T(8,128)(2,1)S(1)} async-done(((bf16[32,64,256]{2,1,0:T(8,128)(2,1)}), bf16[32,64,256]{2,1,0:T(8,128)(2,1)S(1)}, u32[]{:S(2)}, u32[]{:S(2)}) %all-to-all-start.1) | async-done | bytes 1048608 | tf_op jit(solution)/shard_map/all_to_all | solution.py:398
  129.7 0.0 copy-done.4
  129.7 0.0 copy-done.6
  129.7 0.0 copy-start.1
  129.7 1.0 copy-done.1
  130.7 13.7 %image.3 = (f32[4096,256]{1,0:T(8,128)}, f32[1024,128]{1,0:T(8,128)}) custom-call(s32[32]{0:T(128)} %bitcast.21, f32[4096,256]{1,0:T(8,128)} %near.3.base_ref, f32[4096,256]{1,0:T(8,128)} %get-tuple-element.11.res_ref.refs_1_, bf16[32,64,256]{2,1,0:T(8,128)(2,1)} %copy-done.1, bf16[32,1,64,64]{3,2,1,0:T(8,128)(2,1)} %coupling_ref.3, ...), custom_call_target="tpu_custom_call" | custom-call | tf_op jit(solution)/shard_map/image/pallas_call | solution.py:298
  144.4 25.3 %sum_over_devices.3.both_ref = f32[1024,128]{1,0:T(8,128)} custom-call(f32[1024,128]{1,0:T(8,128)} %get-tuple-element.14.part_ref), custom_call_target="tpu_custom_call" | custom-call | tf_op jit(solution)/shard_map/sum_over_devices/pallas_call | solution.py:133
  169.8 12.4 %solve.3.refs_3_ = f32[256,256]{1,0:T(8,128)} custom-call(f32[1024,128]{1,0:T(8,128)} %sum_over_devices.3.both_ref), custom_call_target="tpu_custom_call" | custom-call | tf_op jit(solution)/shard_map/solve/pallas_call | solution.py:188
  182.2 12.2 %last_update.1 = (f32[4096,256]{1,0:T(8,128)}, f32[4096,256]{1,0:T(8,128)}) custom-call(f32[4096,256]{1,0:T(8,128)} %refs_0_.1, f32[4096,256]{1,0:T(8,128)} %get-tuple-element.11.res_ref.refs_1_, f32[256,256]{1,0:T(8,128)} %solve.2.alpha_ref.refs_2_, f32[256,256]{1,0:T(8,128)} %solve.3.refs_3_, f32[4096,256]{1,0:T(8,128)} %get-tuple-element.15.refs_4_), custom_call_target="tpu_custom_call" | custom-call | tf_op jit(solution)/shard_map/last_update/pallas_call | solution.py:370
  (2 shorter events, 0.0 us)
Async XLA Ops:
  0.6 3.1 %copy-start.3 = (bf16[4096,64]{0,1:T(8,128)(2,1)S(1)}, bf16[4096,64]{0,1:T(8,128)(2,1)}, u32[]{:S(2)}) copy-start(bf16[4096,64]{0,1:T(8,128)(2,1)} %param.9) | copy-start | bytes 1572868
  3.8 8.2 %copy-start = (bf16[4096,256]{1,0:T(8,128)(2,1)}, bf16[4096,256]{1,0:T(8,128)(2,1)S(1)}, u32[]{:S(2)}) copy-start(bf16[4096,256]{1,0:T(8,128)(2,1)S(1)} %convert_element_type.6.vb_ref) | copy-start | bytes 6291460
  5.8 30.1 %all-to-all-start = ((bf16[32,64,256]{2,1,0:T(8,128)(2,1)}), bf16[32,64,256]{2,1,0:T(8,128)(2,1)S(1)}, u32[]{:S(2)}, u32[]{:S(2)}) async-start(bf16[32,64,256]{2,1,0:T(8,128)(2,1)} %gather_fusion), calls=%async_computation | async-start | bytes 2097152 | tf_op jit(solution)/shard_map/all_to_all | solution.py:398
  12.0 13.8 %collective-permute-start.1 = (bf16[256,256]{1,0:T(8,128)(2,1)S(1)}, bf16[256,256]{1,0:T(8,128)(2,1)S(1)}, u32[]{:S(2)}, u32[]{:S(2)}) collective-permute-start(bf16[256,256]{1,0:T(8,128)(2,1)S(1)} %get-tuple-element.18), channel_id=1, source_target_pairs={{1,0},{2,1},{3,2},{4,3},{5,4},{6,5},{7,6},{0,7},{9,8},{10,9},{11,1... | collective-permute-start | bytes 393224 | tf_op jit(solution)/shard_map/ppermute | solution.py:20
  12.4 13.4 %collective-permute-start = (bf16[256,256]{1,0:T(8,128)(2,1)S(1)}, bf16[256,256]{1,0:T(8,128)(2,1)S(1)}, u32[]{:S(2)}, u32[]{:S(2)}) collective-permute-start(bf16[256,256]{1,0:T(8,128)(2,1)S(1)} %get-tuple-element.19), channel_id=1, source_target_pairs={{0,1},{1,2},{2,3},{3,4},{4,5},{5,6},{6,7},{7,0},{8,9},{9,10},{10,1... | collective-permute-start | bytes 393224 | tf_op jit(solution)/shard_map/ppermute | solution.py:20
  25.8 10.1 %copy-start.5 = (bf16[256,256]{1,0:T(8,128)(2,1)}, bf16[256,256]{1,0:T(8,128)(2,1)S(1)}, u32[]{:S(2)}) copy-start(bf16[256,256]{1,0:T(8,128)(2,1)S(1)} %collective-permute-done.1.after_ref) | copy-start | bytes 393220
  25.8 10.1 %copy-start.7 = (bf16[256,256]{1,0:T(8,128)(2,1)}, bf16[256,256]{1,0:T(8,128)(2,1)S(1)}, u32[]{:S(2)}) copy-start(bf16[256,256]{1,0:T(8,128)(2,1)S(1)} %collective-permute-done.before_ref) | copy-start | bytes 393220
  35.9 1.0 copy-start.2
  100.9 28.8 %all-to-all-start.1 = ((bf16[32,64,256]{2,1,0:T(8,128)(2,1)}), bf16[32,64,256]{2,1,0:T(8,128)(2,1)S(1)}, u32[]{:S(2)}, u32[]{:S(2)}) async-start(bf16[32,64,256]{2,1,0:T(8,128)(2,1)} %gather_fusion.1), calls=%async_computation.1 | async-start | bytes 2097152 | tf_op jit(solution)/shard_map/all_to_all | solution.py:398
  106.8 13.8 %collective-permute-start.3 = (bf16[256,256]{1,0:T(8,128)(2,1)S(1)}, bf16[256,256]{1,0:T(8,128)(2,1)S(1)}, u32[]{:S(2)}, u32[]{:S(2)}) collective-permute-start(bf16[256,256]{1,0:T(8,128)(2,1)S(1)} %get-tuple-element.16), channel_id=1, source_target_pairs={{1,0},{2,1},{3,2},{4,3},{5,4},{6,5},{7,6},{0,7},{9,8},{10,9},{11,1... | collective-permute-start | bytes 393224 | tf_op jit(solution)/shard_map/ppermute | solution.py:20
  107.2 13.4 %collective-permute-start.2 = (bf16[256,256]{1,0:T(8,128)(2,1)S(1)}, bf16[256,256]{1,0:T(8,128)(2,1)S(1)}, u32[]{:S(2)}, u32[]{:S(2)}) collective-permute-start(bf16[256,256]{1,0:T(8,128)(2,1)S(1)} %get-tuple-element.17), channel_id=1, source_target_pairs={{0,1},{1,2},{2,3},{3,4},{4,5},{5,6},{6,7},{7,0},{8,9},{9,10},{10,1... | collective-permute-start | bytes 393224 | tf_op jit(solution)/shard_map/ppermute | solution.py:20
  120.6 9.2 %copy-start.4 = (bf16[256,256]{1,0:T(8,128)(2,1)}, bf16[256,256]{1,0:T(8,128)(2,1)S(1)}, u32[]{:S(2)}) copy-start(bf16[256,256]{1,0:T(8,128)(2,1)S(1)} %collective-permute-done.3.after_ref) | copy-start | bytes 393220
  120.6 9.1 %copy-start.6 = (bf16[256,256]{1,0:T(8,128)(2,1)}, bf16[256,256]{1,0:T(8,128)(2,1)S(1)}, u32[]{:S(2)}) copy-start(bf16[256,256]{1,0:T(8,128)(2,1)S(1)} %collective-permute-done.2.before_ref) | copy-start | bytes 393220
  129.7 1.0 copy-start.1

commit v5 on v4

--- a/solution.py
+++ b/solution.py
@@ -195,6 +195,7 @@
 
 
 TILE = 512
+IMAGE_TILE = 1024
 WHOLE = pl.BlockSpec(memory_space=pltpu.VMEM)
 
 
@@ -211,8 +212,8 @@
     return lax.dot_general(a, b, (((0,), (0,)), ((), ())), preferred_element_type=jnp.float32)
 
 
-def tiles(width):
-    return pl.BlockSpec((TILE, width), lambda i: (i, 0))
+def tiles(width, tile=TILE):
+    return pl.BlockSpec((tile, width), lambda i: (i, 0))
 
 
 def near_kernel(near_ref, vb_ref, res_ref, out_ref, ext):
@@ -249,7 +250,7 @@
     i = pl.program_id(0)
     width = base_ref.shape[1]
     half = width // 2
-    leaves = TILE // LEAF
+    leaves = IMAGE_TILE // LEAF
 
     @pl.when(i == 0)
     def _():
@@ -263,11 +264,11 @@
         far = tdot16(target_ref[:, l * LEAF : (l + 1) * LEAF], trans.astype(jnp.bfloat16))
         image_ref[l * LEAF : (l + 1) * LEAF] = base_ref[l * LEAF : (l + 1) * LEAF] + far
 
-    @pl.when(i < NEAR // TILE)
+    @pl.when(i < NEAR // IMAGE_TILE)
     def _():
         image_ref[...] += dot16(first_ref[...], before_ref[...])
 
-    @pl.when(i >= pl.num_programs(0) - NEAR // TILE)
+    @pl.when(i >= pl.num_programs(0) - NEAR // IMAGE_TILE)
     def _():
         image_ref[...] += dot16(last_ref[...], after_ref[...])
 
@@ -292,29 +293,29 @@
 def image_and_sums(readers, base, residual, incoming, coupling, target_t, near_blocks, before, after):
     rows, width = residual.shape
     leaves, fanout, rank, _ = coupling.shape
-    step = TILE // LEAF
-    edge, steps = NEAR // TILE, rows // TILE
+    step = IMAGE_TILE // LEAF
+    edge, steps = NEAR // IMAGE_TILE, rows // IMAGE_TILE
     last_column = near_blocks.shape[1] // HALO - 1
     return pl.pallas_call(
         functools.partial(image_kernel, fanout),
-        grid=(rows // TILE,),
+        grid=(rows // IMAGE_TILE,),
         out_shape=(
             jax.ShapeDtypeStruct(residual.shape, jnp.float32),
             jax.ShapeDtypeStruct((4 * width, width // 2), jnp.float32),
         ),
         in_specs=[
             pl.BlockSpec(memory_space=pltpu.SMEM),
-            tiles(width),
-            tiles(width),
+            tiles(width, IMAGE_TILE),
+            tiles(width, IMAGE_TILE),
             WHOLE,
             pl.BlockSpec((step, fanout, rank, rank), lambda i: (i, 0, 0, 0)),
-            pl.BlockSpec((rank, TILE), lambda i: (0, i)),
-            pl.BlockSpec((TILE, HALO), lambda i: (jnp.minimum(i, edge - 1), 0)),
-            pl.BlockSpec((TILE, HALO), lambda i: (jnp.maximum(i, steps - edge), last_column)),
+            pl.BlockSpec((rank, IMAGE_TILE), lambda i: (0, i)),
+            pl.BlockSpec((IMAGE_TILE, HALO), lambda i: (jnp.minimum(i, edge - 1), 0)),
+            pl.BlockSpec((IMAGE_TILE, HALO), lambda i: (jnp.maximum(i, steps - edge), last_column)),
             WHOLE,
             WHOLE,
         ],
-        out_specs=(tiles(width), pl.BlockSpec((4 * width, width // 2), lambda i: (0, 0))),
+        out_specs=(tiles(width, IMAGE_TILE), pl.BlockSpec((4 * width, width // 2), lambda i: (0, 0))),
         scratch_shapes=[pltpu.VMEM((width, width), jnp.float32)],
         name="image",
     )(readers, base, residual, incoming, coupling, target_t, near_blocks, near_blocks, before, after)

time: 197 us -> 193 us (0.980)
  Pallas kernels: 149 us -> 146 us
    pallas_call x2, Pallas kernels: 27.4 us -> 24.1 us  [image_and_sums(): pl.pallas_call(functools.partial(image_kernel, fanout), grid=(rows // IMA...]
  transfers between devices with their start and end apart: 6 -> 6, of which waited for: 2 -> 2; matrix products, arithmetic and copies ran while one was open for 1% -> 1% of each run, Pallas kernels for 12% -> 13%
where the time goes in v5:
time: 193 us; the launch traced here: 191 us
  Pallas kernels  146 us (76%)
  waiting for transfers between devices  19.2 us (10%)
  starting transfers between devices  14.6 us (8%)
  local copies, waits for them, and re-layouts  7.4 us (4%)
  other arithmetic  3.11 us (2%)
    pallas_call x2, Pallas kernels, sum_over_devices(): pl.pallas_call(functools.partial(sum_kernel, n, n_blk), out_shape=jax.Sha...  50.6 us
    pallas_call x2, Pallas kernels, solve(): pl.pallas_call(solve_kernel, out_shape=jax.ShapeDtypeStruct((width, width...  24.8 us
    pallas_call x2, Pallas kernels, image_and_sums(): pl.pallas_call(functools.partial(image_kernel, fanout), grid=(rows // IMA...  24.1 us
    pallas_call x2, Pallas kernels, near_base(): pl.pallas_call(near_kernel, grid=(rows // TILE,), out_shape=jax.ShapeDtyp...  24 us
    all_to_all x2, waiting for transfers between devices, shards(): lax.all_to_all(outgoing, ('wide', 'blk'), split_axis=0, concat_axis=0, ti...  19.2 us
    pallas_call x1, Pallas kernels, last_update(): pl.pallas_call(functools.partial(last_kernel, count), grid=(rows // TILE,...  12.2 us
    all_to_all x2, starting transfers between devices, shards(): lax.all_to_all(outgoing, ('wide', 'blk'), split_axis=0, concat_axis=0, ti...  11 us
    pallas_call x1, Pallas kernels, update(): pl.pallas_call(update_kernel, grid=(rows // TILE,), out_shape=(jax.ShapeD...  9.78 us
  transfers between devices with their start and end apart: 6, of which 2 were waited for; matrix products, arithmetic and copies ran while one was open for 1% of the time, Pallas kernels for 13%

profile of v5, /device:TPU:29, one launch (start us, length us, event | category | flops | bytes accessed | tf_op | source)
XLA Modules:
  0.0 191.1 jit_solution(17421574546352011091)
XLA Ops:
  0.6 0.0 copy-start.3
  0.6 0.7 fusion.2
  1.4 2.4 %convert_element_type.6.vb_ref = bf16[4096,256]{1,0:T(8,128)(2,1)S(1)} convert(f32[4096,256]{1,0:T(8,128)} %refs_0_.1) | non-fusion elementwise | flops 1048576 | bytes 6291456 | tf_op jit(solution)/shard_map/convert_element_type | solution.py:392
  3.8 0.0 copy-start
  3.8 0.0 copy-done.3
  3.8 0.4 convolution_convert_fusion
  4.2 1.6 gather_fusion
  5.8 6.1 %all-to-all-start = ((bf16[32,64,256]{2,1,0:T(8,128)(2,1)}), bf16[32,64,256]{2,1,0:T(8,128)(2,1)S(1)}, u32[]{:S(2)}, u32[]{:S(2)}) async-start(bf16[32,64,256]{2,1,0:T(8,128)(2,1)} %gather_fusion), calls=%async_computation | async-start | bytes 2097152 | tf_op jit(solution)/shard_map/all_to_all | solution.py:399
  12.0 0.0 copy-done
  12.0 0.4 collective-permute-start.1
  12.4 1.4 collective-permute-start
  13.8 12.0 %near.2.base_ref = f32[4096,256]{1,0:T(8,128)} custom-call(bf16[4096,1536]{1,0:T(8,128)(2,1)} %last_ref.3, bf16[4096,256]{1,0:T(8,128)(2,1)} %copy-done, f32[4096,256]{1,0:T(8,128)} %refs_0_.1), custom_call_target="tpu_custom_call" | custom-call | flops 3221225472 | bytes 20971520 | tf_op jit(solution)/shard_map/near/pallas_call | solution.py:235
  25.8 0.0 collective-permute-done.1.after_ref
  25.8 0.0 copy-start.5
  25.8 0.0 collective-permute-done.before_ref
  25.8 0.0 copy-start.7
  25.8 10.1 %all-to-all-done.incoming_ref = bf16[32,64,256]{2,1,0:T(8,128)(2,1)S(1)} async-done(((bf16[32,64,256]{2,1,0:T(8,128)(2,1)}), bf16[32,64,256]{2,1,0:T(8,128)(2,1)S(1)}, u32[]{:S(2)}, u32[]{:S(2)}) %all-to-all-start) | async-done | bytes 1048608 | tf_op jit(solution)/shard_map/all_to_all | solution.py:399
  35.9 0.0 copy-start.2
  35.9 0.0 copy-done.5
  35.9 0.0 copy-done.7
  35.9 1.0 copy-done.2
  36.9 12.0 %image.2 = (f32[4096,256]{1,0:T(8,128)}, f32[1024,128]{1,0:T(8,128)}) custom-call(s32[32]{0:T(128)} %bitcast.20, f32[4096,256]{1,0:T(8,128)} %near.2.base_ref, f32[4096,256]{1,0:T(8,128)} %refs_0_.1, bf16[32,64,256]{2,1,0:T(8,128)(2,1)} %copy-done.2, bf16[32,1,64,64]{3,2,1,0:T(8,128)(2,1)} %coupling_ref.3, bf16[64,4096]{1,0:T(8,128)(2,1)} %bitcast.17, ...), custom_call_target="tpu_custom_call" | custom-call | tf_op jit(solution)/shard_map/image/pallas_call | solution.py:299
  48.9 25.3 %sum_over_devices.2.both_ref = f32[1024,128]{1,0:T(8,128)} custom-call(f32[1024,128]{1,0:T(8,128)} %get-tuple-element.10.part_ref), custom_call_target="tpu_custom_call" | custom-call | tf_op jit(solution)/shard_map/sum_over_devices/pallas_call | solution.py:133
  74.2 12.4 %solve.2.alpha_ref.refs_2_ = f32[256,256]{1,0:T(8,128)} custom-call(f32[1024,128]{1,0:T(8,128)} %sum_over_devices.2.both_ref), custom_call_target="tpu_custom_call" | custom-call | tf_op jit(solution)/shard_map/solve/pallas_call | solution.py:188
  86.6 9.8 %update.1 = (f32[4096,256]{1,0:T(8,128)}, bf16[4096,256]{1,0:T(8,128)(2,1)}, bf16[32,64,256]{2,1,0:T(8,128)(2,1)}) custom-call(f32[4096,256]{1,0:T(8,128)} %refs_0_.1, f32[4096,256]{1,0:T(8,128)} %get-tuple-element.9.image_ref, f32[256,256]{1,0:T(8,128)} %solve.2.alpha_ref.refs_2_, bf16[64,4096]{1,0:T(8,128)(2,1)} %bitcast.19), custom_call_target="tpu_custom_call" | custom-call | tf_op jit(solution)/shard_map/update/pallas_call | solution.py:343
  96.4 2.8 %gather_fusion.1 = bf16[32,64,256]{2,1,0:T(8,128)(2,1)} fusion(bf16[32,64,256]{2,1,0:T(8,128)(2,1)} %get-tuple-element.13, s32[1024]{0:T(1024)S(1)} %pad_clamp_fusion), kind=kCustom, calls=%fused_computation.1 | custom fusion | bytes 2097280 | tf_op jit(solution)/shard_map/gather | solution.py:398
  99.2 4.9 %all-to-all-start.1 = ((bf16[32,64,256]{2,1,0:T(8,128)(2,1)}), bf16[32,64,256]{2,1,0:T(8,128)(2,1)S(1)}, u32[]{:S(2)}, u32[]{:S(2)}) async-start(bf16[32,64,256]{2,1,0:T(8,128)(2,1)} %gather_fusion.1), calls=%async_computation.1 | async-start | bytes 2097152 | tf_op jit(solution)/shard_map/all_to_all | solution.py:399
  104.1 1.0 fusion.3
  105.1 0.4 collective-permute-start.3
  105.5 1.4 collective-permute-start.2
  106.9 12.0 %near.3.base_ref = f32[4096,256]{1,0:T(8,128)} custom-call(bf16[4096,1536]{1,0:T(8,128)(2,1)} %last_ref.3, bf16[4096,256]{1,0:T(8,128)(2,1)} %get-tuple-element.12.vb_ref, f32[4096,256]{1,0:T(8,128)} %get-tuple-element.11.res_ref.refs_1_), custom_call_target="tpu_custom_call" | custom-call | flops 3221225472 | bytes 20971520 | tf_op jit(solution)/shard_map/near/pallas_call | solution.py:235
  118.9 0.0 collective-permute-done.3.after_ref
  118.9 0.0 copy-start.4
  118.9 0.0 collective-permute-done.2.before_ref
  118.9 0.0 copy-start.6
  118.9 9.1 %all-to-all-done.1.incoming_ref = bf16[32,64,256]{2,1,0:T(8,128)(2,1)S(1)} async-done(((bf16[32,64,256]{2,1,0:T(8,128)(2,1)}), bf16[32,64,256]{2,1,0:T(8,128)(2,1)S(1)}, u32[]{:S(2)}, u32[]{:S(2)}) %all-to-all-start.1) | async-done | bytes 1048608 | tf_op jit(solution)/shard_map/all_to_all | solution.py:399
  128.0 0.0 copy-done.4
  128.0 0.0 copy-done.6
  128.0 0.0 copy-start.1
  128.0 1.0 copy-done.1
  129.0 12.1 %image.3 = (f32[4096,256]{1,0:T(8,128)}, f32[1024,128]{1,0:T(8,128)}) custom-call(s32[32]{0:T(128)} %bitcast.21, f32[4096,256]{1,0:T(8,128)} %near.3.base_ref, f32[4096,256]{1,0:T(8,128)} %get-tuple-element.11.res_ref.refs_1_, bf16[32,64,256]{2,1,0:T(8,128)(2,1)} %copy-done.1, bf16[32,1,64,64]{3,2,1,0:T(8,128)(2,1)} %coupling_ref.3, ...), custom_call_target="tpu_custom_call" | custom-call | tf_op jit(solution)/shard_map/image/pallas_call | solution.py:299
  141.1 25.3 %sum_over_devices.3.both_ref = f32[1024,128]{1,0:T(8,128)} custom-call(f32[1024,128]{1,0:T(8,128)} %get-tuple-element.14.part_ref), custom_call_target="tpu_custom_call" | custom-call | tf_op jit(solution)/shard_map/sum_over_devices/pallas_call | solution.py:133
  166.5 12.4 %solve.3.refs_3_ = f32[256,256]{1,0:T(8,128)} custom-call(f32[1024,128]{1,0:T(8,128)} %sum_over_devices.3.both_ref), custom_call_target="tpu_custom_call" | custom-call | tf_op jit(solution)/shard_map/solve/pallas_call | solution.py:188
  178.9 12.2 %last_update.1 = (f32[4096,256]{1,0:T(8,128)}, f32[4096,256]{1,0:T(8,128)}) custom-call(f32[4096,256]{1,0:T(8,128)} %refs_0_.1, f32[4096,256]{1,0:T(8,128)} %get-tuple-element.11.res_ref.refs_1_, f32[256,256]{1,0:T(8,128)} %solve.2.alpha_ref.refs_2_, f32[256,256]{1,0:T(8,128)} %solve.3.refs_3_, f32[4096,256]{1,0:T(8,128)} %get-tuple-element.15.refs_4_), custom_call_target="tpu_custom_call" | custom-call | tf_op jit(solution)/shard_map/last_update/pallas_call | solution.py:371
  (2 shorter events, 0.0 us)
Async XLA Ops:
  0.6 3.1 %copy-start.3 = (bf16[4096,64]{0,1:T(8,128)(2,1)S(1)}, bf16[4096,64]{0,1:T(8,128)(2,1)}, u32[]{:S(2)}) copy-start(bf16[4096,64]{0,1:T(8,128)(2,1)} %param.9) | copy-start | bytes 1572868
  3.8 8.2 %copy-start = (bf16[4096,256]{1,0:T(8,128)(2,1)}, bf16[4096,256]{1,0:T(8,128)(2,1)S(1)}, u32[]{:S(2)}) copy-start(bf16[4096,256]{1,0:T(8,128)(2,1)S(1)} %convert_element_type.6.vb_ref) | copy-start | bytes 6291460
  5.8 30.1 %all-to-all-start = ((bf16[32,64,256]{2,1,0:T(8,128)(2,1)}), bf16[32,64,256]{2,1,0:T(8,128)(2,1)S(1)}, u32[]{:S(2)}, u32[]{:S(2)}) async-start(bf16[32,64,256]{2,1,0:T(8,128)(2,1)} %gather_fusion), calls=%async_computation | async-start | bytes 2097152 | tf_op jit(solution)/shard_map/all_to_all | solution.py:399
  12.0 13.8 %collective-permute-start.1 = (bf16[256,256]{1,0:T(8,128)(2,1)S(1)}, bf16[256,256]{1,0:T(8,128)(2,1)S(1)}, u32[]{:S(2)}, u32[]{:S(2)}) collective-permute-start(bf16[256,256]{1,0:T(8,128)(2,1)S(1)} %get-tuple-element.18), channel_id=1, source_target_pairs={{1,0},{2,1},{3,2},{4,3},{5,4},{6,5},{7,6},{0,7},{9,8},{10,9},{11,1... | collective-permute-start | bytes 393224 | tf_op jit(solution)/shard_map/ppermute | solution.py:20
  12.4 13.4 %collective-permute-start = (bf16[256,256]{1,0:T(8,128)(2,1)S(1)}, bf16[256,256]{1,0:T(8,128)(2,1)S(1)}, u32[]{:S(2)}, u32[]{:S(2)}) collective-permute-start(bf16[256,256]{1,0:T(8,128)(2,1)S(1)} %get-tuple-element.19), channel_id=1, source_target_pairs={{0,1},{1,2},{2,3},{3,4},{4,5},{5,6},{6,7},{7,0},{8,9},{9,10},{10,1... | collective-permute-start | bytes 393224 | tf_op jit(solution)/shard_map/ppermute | solution.py:20
  25.8 10.1 %copy-start.5 = (bf16[256,256]{1,0:T(8,128)(2,1)}, bf16[256,256]{1,0:T(8,128)(2,1)S(1)}, u32[]{:S(2)}) copy-start(bf16[256,256]{1,0:T(8,128)(2,1)S(1)} %collective-permute-done.1.after_ref) | copy-start | bytes 393220
  25.8 10.1 %copy-start.7 = (bf16[256,256]{1,0:T(8,128)(2,1)}, bf16[256,256]{1,0:T(8,128)(2,1)S(1)}, u32[]{:S(2)}) copy-start(bf16[256,256]{1,0:T(8,128)(2,1)S(1)} %collective-permute-done.before_ref) | copy-start | bytes 393220
  35.9 1.0 copy-start.2
  99.2 28.8 %all-to-all-start.1 = ((bf16[32,64,256]{2,1,0:T(8,128)(2,1)}), bf16[32,64,256]{2,1,0:T(8,128)(2,1)S(1)}, u32[]{:S(2)}, u32[]{:S(2)}) async-start(bf16[32,64,256]{2,1,0:T(8,128)(2,1)} %gather_fusion.1), calls=%async_computation.1 | async-start | bytes 2097152 | tf_op jit(solution)/shard_map/all_to_all | solution.py:399
  105.1 13.8 %collective-permute-start.3 = (bf16[256,256]{1,0:T(8,128)(2,1)S(1)}, bf16[256,256]{1,0:T(8,128)(2,1)S(1)}, u32[]{:S(2)}, u32[]{:S(2)}) collective-permute-start(bf16[256,256]{1,0:T(8,128)(2,1)S(1)} %get-tuple-element.16), channel_id=1, source_target_pairs={{1,0},{2,1},{3,2},{4,3},{5,4},{6,5},{7,6},{0,7},{9,8},{10,9},{11,1... | collective-permute-start | bytes 393224 | tf_op jit(solution)/shard_map/ppermute | solution.py:20
  105.5 13.4 %collective-permute-start.2 = (bf16[256,256]{1,0:T(8,128)(2,1)S(1)}, bf16[256,256]{1,0:T(8,128)(2,1)S(1)}, u32[]{:S(2)}, u32[]{:S(2)}) collective-permute-start(bf16[256,256]{1,0:T(8,128)(2,1)S(1)} %get-tuple-element.17), channel_id=1, source_target_pairs={{0,1},{1,2},{2,3},{3,4},{4,5},{5,6},{6,7},{7,0},{8,9},{9,10},{10,1... | collective-permute-start | bytes 393224 | tf_op jit(solution)/shard_map/ppermute | solution.py:20
  118.9 9.2 %copy-start.4 = (bf16[256,256]{1,0:T(8,128)(2,1)}, bf16[256,256]{1,0:T(8,128)(2,1)S(1)}, u32[]{:S(2)}) copy-start(bf16[256,256]{1,0:T(8,128)(2,1)S(1)} %collective-permute-done.3.after_ref) | copy-start | bytes 393220
  118.9 9.1 %copy-start.6 = (bf16[256,256]{1,0:T(8,128)(2,1)}, bf16[256,256]{1,0:T(8,128)(2,1)S(1)}, u32[]{:S(2)}) copy-start(bf16[256,256]{1,0:T(8,128)(2,1)S(1)} %collective-permute-done.2.before_ref) | copy-start | bytes 393220
  128.0 1.0 copy-start.1
